TPU v7x, 512 devices: a whole 4x4x16 slice. The times are simulated.
512 devices in a mesh: section: 64 (over x, y, z_hi), seq: 8 (over z_lo, core).
Axes of the slice: x: 4, y: 4, z: 16 (z_hi: 4, z_lo: 4; z = z_hi * 4 + z_lo), core: 2. Of those that a mesh axis runs over, the one named last changes fastest.
Arguments:
- section_input: bfloat16 [64, 1024, 4096], P('section', 'seq'), may hold values from -6 to 6
- norm_gain: float32 [64, 4096], P('section'), may hold values from 0.5 to 1.5
- w_query: bfloat16 [64, 4096, 1024], P('section', 'seq'), may hold values from -1 to 1
- w_keyval: bfloat16 [64, 4096, 256], P('section', 'seq'), may hold values from -1 to 1
- w_out: bfloat16 [64, 1024, 4096], P('section', None, 'seq'), may hold values from -0.1875 to 0.1875
- down_grads: bfloat16 [64, 4096, 128], P('section', 'seq'), may hold values from -6 to 6
- up_grads: bfloat16 [64, 4096, 128], P('section', 'seq'), may hold values from -6 to 6
Outputs:
- section_output: bfloat16 [64, 1024, 4096], P('section', 'seq')
- grad_sum: bfloat16 [64, 4096, 128], P('section', 'seq')
All inputs are finite; a program needn't handle non-finite values.
Results may differ from a plain program's by a relative error of at most 0.015.
Values may be sent and summed in bfloat16 or wider, within the bound.
No kernel may reach another device: no remote copies, remote signals or barrier semaphores. Data moves between devices by JAX's collectives and lax.ppermute only.
A program may use at most 64 MiB of HBM per device.

v0:
```python
import math

import jax
import jax.numpy as jnp
from jax import lax
from jax.sharding import PartitionSpec as P


def from_behind(x, axis, by):
    size = lax.axis_size(axis)
    pairs = [(i, i + by) for i in range(size) if 0 <= i + by < size]
    return lax.ppermute(x, axis, pairs)


def from_partner(x, axis, apart):
    return lax.ppermute(x, axis, [(i, i ^ 1 << apart) for i in range(lax.axis_size(axis))])


def rotate(values, positions):
    halfway = values.shape[1] // 2
    frequency = 10000.0 ** (-(jnp.arange(halfway, dtype=jnp.float32) * 2.0 / values.shape[1]))
    angles = positions[:, None] * frequency[None, :]
    cosine = jnp.cos(angles)
    sine_part = jnp.sin(angles)
    leading = values[:, :halfway]
    trailing = values[:, halfway:]
    return jnp.concatenate(
        [leading * cosine - trailing * sine_part, trailing * cosine + leading * sine_part], axis=1
    )


def attend_block(queries, key_rows, value_rows, first_row, block_rows):
    query_block = queries[first_row : first_row + block_rows]
    scale_factor = 1.0 / math.sqrt(queries.shape[1])
    scores = (
        lax.dot_general(
            query_block, key_rows, (((1,), (1,)), ((), ())), preferred_element_type=jnp.float32
        )
        * scale_factor
    )
    row_ids = first_row + jnp.arange(block_rows, dtype=jnp.int32)[:, None]
    col_ids = jnp.arange(key_rows.shape[0], dtype=jnp.int32)[None, :]
    scores = jnp.where(col_ids <= row_ids, scores, jnp.float32(-1e30))
    highest = jnp.max(scores, axis=1, keepdims=True)
    raised = jnp.exp(scores - highest)
    probs = (raised / jnp.sum(raised, axis=1, keepdims=True)).astype(jnp.bfloat16)
    return jnp.dot(probs, value_rows, preferred_element_type=jnp.float32).astype(jnp.bfloat16)


def shards(section_input, norm_gain, w_query, w_keyval, w_out, down_grads, up_grads):
    section_rows = section_input[0]
    widened = section_rows.astype(jnp.float32)
    normed = (
        widened
        * lax.rsqrt(jnp.mean(widened * widened, axis=1, keepdims=True) + 1e-05)
        * norm_gain[0][None, :]
    ).astype(jnp.bfloat16)
    columns = lax.all_to_all(normed, "seq", split_axis=1, concat_axis=0, tiled=True)
    query_weight = w_query[0]
    keyval_weight = w_keyval[0]
    output_weight = w_out[0]
    head_size = keyval_weight.shape[1] // 2
    weight_slab = query_weight
    query_cols = lax.psum_scatter(
        jnp.einsum("sd,dc->cs", columns, weight_slab, preferred_element_type=jnp.float32).astype(
            jnp.bfloat16
        ),
        "seq",
        scatter_dimension=0,
        tiled=True,
    ).astype(jnp.float32)
    keyval = lax.psum(
        jnp.dot(columns, keyval_weight, preferred_element_type=jnp.float32).astype(jnp.bfloat16),
        "seq",
    ).astype(jnp.float32)
    length = columns.shape[0]
    positions = jnp.arange(length, dtype=jnp.float32)
    queries = rotate(query_cols.T, positions).astype(jnp.bfloat16)
    key_rows = rotate(keyval[:, :head_size], positions).astype(jnp.bfloat16)
    value_rows = keyval[:, head_size:].astype(jnp.bfloat16)
    block_rows = min(512, length)
    blocks_out = [
        attend_block(queries, key_rows, value_rows, first_row, block_rows)
        for first_row in range(0, length, block_rows)
    ]
    head_out = jnp.concatenate(blocks_out, axis=0)
    weight_slab = output_weight
    attn_cols = jnp.dot(
        lax.all_gather(head_out, "seq", axis=1, tiled=True),
        weight_slab,
        preferred_element_type=jnp.float32,
    )
    attn_rows = lax.all_to_all(
        attn_cols.astype(jnp.bfloat16), "seq", split_axis=0, concat_axis=1, tiled=True
    )
    result = (widened + attn_rows.astype(jnp.float32)).astype(jnp.bfloat16)
    parity = lax.axis_index("section") % 2
    downward = from_behind(jnp.where(parity == 0, result, jnp.zeros_like(result)), "section", 1)
    upward = from_behind(jnp.where(parity == 1, result, jnp.zeros_like(result)), "section", -1)
    received = downward + upward
    levels = lax.axis_size("section").bit_length() - 1
    carried = up_grads[0]
    for bit_level in range(levels):
        carried = from_partner(carried, "section", bit_level)
    grad_total = (down_grads[0].astype(jnp.float32) + carried.astype(jnp.float32)).astype(
        jnp.bfloat16
    )
    return (received[None], grad_total[None])


def solution(mesh):
    return jax.shard_map(
        shards,
        mesh=mesh,
        in_specs=(
            P("section", "seq", None),
            P("section", None),
            P("section", "seq", None),
            P("section", "seq", None),
            P("section", None, "seq"),
            P("section", "seq", None),
            P("section", "seq", None),
        ),
        out_specs=(P("section", "seq", None), P("section", "seq", None)),
        check_vma=False,
    )
```

profile of v0, /device:TPU:22, one launch (start us, length us, event | category | flops | bytes accessed | tf_op | source)
XLA Modules:
  0.0 444.4 jit_solution(17630881499146507036)
XLA Ops:
  7.2 1.7 copy.15
  11.4 32.5 %all_to_all.29 = bf16[128,8,512]{0,2,1:T(8,128)(2,1)} all-to-all(bf16[128,8,512]{0,2,1:T(8,128)(2,1)S(1)} %multiply_convert_fusion), channel_id=1, replica_groups=mesh['section'=64,'seq'=8] {'seq'}, dimensions={1} | all-to-all | bytes 2097152 | tf_op jit(solution)/shard_map/all_to_all | solution.py:58
  44.0 1.5 copy.16
  45.5 1.2 convolution_convert_fusion.1
  46.8 2.6 convert_bitcast_fusion.1
  49.4 3.9 copy.19
  53.4 76.9 %all-reduce.2.cloned.1.call-done = bf16[1024,256]{1,0:T(8,128)(2,1)} async-done(((bf16[1024,256]{1,0:T(8,128)(2,1)}), bf16[1024,256]{1,0:T(8,128)(2,1)}) %all-reduce.2.cloned.1.call-update) | async-done | bytes 524304 | tf_op jit(solution)/shard_map/psum | solution.py:72
  131.4 47.2 %reduce-scatter.4.cloned.1.call-done = bf16[128,1024]{1,0:T(8,128)(2,1)} async-done(((bf16[1024,1024]{1,0:T(8,128)(2,1)}), bf16[128,1024]{1,0:T(8,128)(2,1)}) %reduce-scatter.4.cloned.1.call-update) | async-done | bytes 262160
  178.6 1.1 copy.20
  179.8 2.4 subtract_convert_fusion
  186.4 42.7 %all-gather.2.cloned.1.call-done = bf16[1024,1024]{1,0:T(8,128)(2,1)} async-done(((bf16[1024,128]{1,0:T(8,128)(2,1)}), bf16[1024,1024]{1,0:T(8,128)(2,1)}) %all-gather.2.cloned.1.call-update) | async-done | bytes 2097168 | tf_op jit(solution)/shard_map/all_gather | solution.py:89
  229.1 3.8 convolution_convert_fusion
  233.0 3.7 all-to-all-start.1
  236.6 26.6 %all-to-all-done.1 = bf16[8,128,512]{2,1,0:T(8,128)(2,1)S(1)} async-done(((bf16[8,128,512]{2,1,0:T(8,128)(2,1)}), bf16[8,128,512]{2,1,0:T(8,128)(2,1)S(1)}, u32[]{:S(2)}, u32[]{:S(2)}) %all-to-all-start.1) | async-done | bytes 1048608 | tf_op jit(solution)/shard_map/all_to_all | solution.py:93
  263.2 1.6 convert_bitcast_fusion
  264.9 2.9 copy.17
  267.8 2.0 broadcast_select_fusion
  269.8 7.7 %collective-permute-start = (bf16[128,4096]{0,1:T(8,128)(2,1)S(1)}, bf16[128,4096]{0,1:T(8,128)(2,1)S(1)}, u32[]{:S(2)}, u32[]{:S(2)}) collective-permute-start(bf16[128,4096]{0,1:T(8,128)(2,1)S(1)} %get-tuple-element.7), channel_id=1, source_target_pairs={{0,8},{8,16},{16,24},{24,32},{32,40},{40,48},{48,56},{56,64},{64,7... | collective-permute-start | bytes 3145736 | tf_op jit(solution)/shard_map/ppermute | solution.py:12
  277.5 3.0 collective-permute-start.1
  280.5 6.8 %collective-permute-start.2 = (bf16[512,128]{1,0:T(8,128)(2,1)S(1)}, bf16[512,128]{1,0:T(8,128)(2,1)S(1)}, u32[]{:S(2)}, u32[]{:S(2)}) collective-permute-start(bf16[512,128]{1,0:T(8,128)(2,1)S(1)} %bitcast.54), channel_id=1, source_target_pairs={{0,8},{8,0},{16,24},{24,16},{32,40},{40,32},{48,56},{56,48},{64,72... | collective-permute-start | bytes 393224 | tf_op jit(solution)/shard_map/ppermute | solution.py:16
  287.2 97.8 %collective-permute-done.2 = bf16[512,128]{1,0:T(8,128)(2,1)S(1)} collective-permute-done((bf16[512,128]{1,0:T(8,128)(2,1)S(1)}, bf16[512,128]{1,0:T(8,128)(2,1)S(1)}, u32[]{:S(2)}, u32[]{:S(2)}) %collective-permute-start.2) | collective-permute-done | bytes 131104 | tf_op jit(solution)/shard_map/ppermute | solution.py:16
  385.1 5.1 %collective-permute-start.3 = (bf16[512,128]{1,0:T(8,128)(2,1)S(1)}, bf16[512,128]{1,0:T(8,128)(2,1)S(1)}, u32[]{:S(2)}, u32[]{:S(2)}) collective-permute-start(bf16[512,128]{1,0:T(8,128)(2,1)S(1)} %collective-permute-done.2), channel_id=1, source_target_pairs={{0,16},{8,24},{16,0},{24,8},{32,48},{40,56},{48,32},{56,40},{64,80... | collective-permute-start | bytes 393224 | tf_op jit(solution)/shard_map/ppermute | solution.py:16
  390.2 13.8 %collective-permute-done.3 = bf16[512,128]{1,0:T(8,128)(2,1)S(1)} collective-permute-done((bf16[512,128]{1,0:T(8,128)(2,1)S(1)}, bf16[512,128]{1,0:T(8,128)(2,1)S(1)}, u32[]{:S(2)}, u32[]{:S(2)}) %collective-permute-start.3) | collective-permute-done | bytes 131104 | tf_op jit(solution)/shard_map/ppermute | solution.py:16
  404.0 2.7 collective-permute-start.4
  406.6 4.2 collective-permute-done.4
  410.8 2.5 collective-permute-start.5
  413.3 5.8 %collective-permute-done.5 = bf16[512,128]{1,0:T(8,128)(2,1)S(1)} collective-permute-done((bf16[512,128]{1,0:T(8,128)(2,1)S(1)}, bf16[512,128]{1,0:T(8,128)(2,1)S(1)}, u32[]{:S(2)}, u32[]{:S(2)}) %collective-permute-start.5) | collective-permute-done | bytes 131104 | tf_op jit(solution)/shard_map/ppermute | solution.py:16
  419.2 2.8 collective-permute-start.6
  422.0 5.4 %collective-permute-done.6 = bf16[512,128]{1,0:T(8,128)(2,1)S(1)} collective-permute-done((bf16[512,128]{1,0:T(8,128)(2,1)S(1)}, bf16[512,128]{1,0:T(8,128)(2,1)S(1)}, u32[]{:S(2)}, u32[]{:S(2)}) %collective-permute-start.6) | collective-permute-done | bytes 131104 | tf_op jit(solution)/shard_map/ppermute | solution.py:16
  427.4 1.9 collective-permute-start.7
  429.3 6.4 %collective-permute-done.7 = bf16[512,128]{1,0:T(8,128)(2,1)S(1)} collective-permute-done((bf16[512,128]{1,0:T(8,128)(2,1)S(1)}, bf16[512,128]{1,0:T(8,128)(2,1)S(1)}, u32[]{:S(2)}, u32[]{:S(2)}) %collective-permute-start.7) | collective-permute-done | bytes 131104 | tf_op jit(solution)/shard_map/ppermute | solution.py:16
  436.5 1.3 copy.18
  (41 shorter events, 8.8 us)
Async XLA Ops:
  7.2 39.6 %copy-start = (bf16[1,512,1024]{2,1,0:T(8,128)(2,1)S(1)}, bf16[1,512,1024]{2,1,0:T(8,128)(2,1)}, u32[]{:S(2)}) copy-start(bf16[1,512,1024]{2,1,0:T(8,128)(2,1)} %param.9) | copy-start | bytes 3145732
  7.2 2.8 copy-start.4
  7.2 123.1 %all-reduce.2.cloned.1.call-start = ((), (), s32[]{:S(2)}) async-start(), calls=%async_computation.3 | async-start | bytes 1048576 | tf_op jit(solution)/shard_map/psum | solution.py:72
  11.4 34.0 %copy-start.2 = (bf16[1,512,256]{2,1,0:T(8,128)(2,1)S(1)}, bf16[1,512,256]{2,1,0:T(8,128)(2,1)}, u32[]{:S(2)}) copy-start(bf16[1,512,256]{2,1,0:T(8,128)(2,1)} %param.10) | copy-start | bytes 786436
  46.7 131.9 %reduce-scatter.4.cloned.1.call-start = ((), (), s32[]{:S(2)}) async-start(), calls=%async_computation.5 | async-start | bytes 2359296
  53.3 175.8 %all-gather.2.cloned.1.call-start = ((), (), s32[]{:S(2)}) async-start(), calls=%async_computation.4 | async-start | bytes 2359296 | tf_op jit(solution)/shard_map/all_gather | solution.py:89
  183.5 1.0 copy-start.1
  185.1 44.0 %copy-start.5 = (bf16[1,1024,512]{2,1,0:T(8,128)(2,1)S(1)}, bf16[1,1024,512]{2,1,0:T(8,128)(2,1)}, u32[]{:S(2)}) copy-start(bf16[1,1024,512]{2,1,0:T(8,128)(2,1)} %param.11) | copy-start | bytes 3145732
  233.0 30.3 %all-to-all-start.1 = ((bf16[8,128,512]{2,1,0:T(8,128)(2,1)}), bf16[8,128,512]{2,1,0:T(8,128)(2,1)S(1)}, u32[]{:S(2)}, u32[]{:S(2)}) async-start(bf16[8,128,512]{2,1,0:T(8,128)(2,1)} %bitcast.53), calls=%async_computation.1 | async-start | bytes 2097152 | tf_op jit(solution)/shard_map/all_to_all | solution.py:93
  267.7 12.7 %copy-start.6 = (bf16[1,512,128]{2,1,0:T(8,128)(2,1)S(1)}, bf16[1,512,128]{2,1,0:T(8,128)(2,1)}, u32[]{:S(2)}) copy-start(bf16[1,512,128]{2,1,0:T(8,128)(2,1)} %param.13) | copy-start | bytes 393220
  267.8 168.0 %copy-start.3 = (bf16[1,512,128]{2,1,0:T(8,128)(2,1)S(1)}, bf16[1,512,128]{2,1,0:T(8,128)(2,1)}, u32[]{:S(2)}) copy-start(bf16[1,512,128]{2,1,0:T(8,128)(2,1)} %param.12) | copy-start | bytes 393220
  269.8 166.6 %collective-permute-start = (bf16[128,4096]{0,1:T(8,128)(2,1)S(1)}, bf16[128,4096]{0,1:T(8,128)(2,1)S(1)}, u32[]{:S(2)}, u32[]{:S(2)}) collective-permute-start(bf16[128,4096]{0,1:T(8,128)(2,1)S(1)} %get-tuple-element.7), channel_id=1, source_target_pairs={{0,8},{8,16},{16,24},{24,32},{32,40},{40,48},{48,56},{56,64},{64,7... | collective-permute-start | bytes 3145736 | tf_op jit(solution)/shard_map/ppermute | solution.py:12
  277.5 159.0 %collective-permute-start.1 = (bf16[128,4096]{0,1:T(8,128)(2,1)S(1)}, bf16[128,4096]{0,1:T(8,128)(2,1)S(1)}, u32[]{:S(2)}, u32[]{:S(2)}) collective-permute-start(bf16[128,4096]{0,1:T(8,128)(2,1)S(1)} %get-tuple-element.6), channel_id=1, source_target_pairs={{8,0},{16,8},{24,16},{32,24},{40,32},{48,40},{56,48},{64,56},{72,6... | collective-permute-start | bytes 3145736 | tf_op jit(solution)/shard_map/ppermute | solution.py:12
  280.5 104.6 %collective-permute-start.2 = (bf16[512,128]{1,0:T(8,128)(2,1)S(1)}, bf16[512,128]{1,0:T(8,128)(2,1)S(1)}, u32[]{:S(2)}, u32[]{:S(2)}) collective-permute-start(bf16[512,128]{1,0:T(8,128)(2,1)S(1)} %bitcast.54), channel_id=1, source_target_pairs={{0,8},{8,0},{16,24},{24,16},{32,40},{40,32},{48,56},{56,48},{64,72... | collective-permute-start | bytes 393224 | tf_op jit(solution)/shard_map/ppermute | solution.py:16
  385.1 18.9 %collective-permute-start.3 = (bf16[512,128]{1,0:T(8,128)(2,1)S(1)}, bf16[512,128]{1,0:T(8,128)(2,1)S(1)}, u32[]{:S(2)}, u32[]{:S(2)}) collective-permute-start(bf16[512,128]{1,0:T(8,128)(2,1)S(1)} %collective-permute-done.2), channel_id=1, source_target_pairs={{0,16},{8,24},{16,0},{24,8},{32,48},{40,56},{48,32},{56,40},{64,80... | collective-permute-start | bytes 393224 | tf_op jit(solution)/shard_map/ppermute | solution.py:16
  404.0 6.8 %collective-permute-start.4 = (bf16[512,128]{1,0:T(8,128)(2,1)S(1)}, bf16[512,128]{1,0:T(8,128)(2,1)S(1)}, u32[]{:S(2)}, u32[]{:S(2)}) collective-permute-start(bf16[512,128]{1,0:T(8,128)(2,1)S(1)} %collective-permute-done.3), channel_id=1, source_target_pairs={{0,32},{8,40},{16,48},{24,56},{32,0},{40,8},{48,16},{56,24},{64,96... | collective-permute-start | bytes 393224 | tf_op jit(solution)/shard_map/ppermute | solution.py:16
  410.8 8.4 %collective-permute-start.5 = (bf16[512,128]{1,0:T(8,128)(2,1)S(1)}, bf16[512,128]{1,0:T(8,128)(2,1)S(1)}, u32[]{:S(2)}, u32[]{:S(2)}) collective-permute-start(bf16[512,128]{1,0:T(8,128)(2,1)S(1)} %collective-permute-done.4), channel_id=1, source_target_pairs={{0,64},{8,72},{16,80},{24,88},{32,96},{40,104},{48,112},{56,120},{... | collective-permute-start | bytes 393224 | tf_op jit(solution)/shard_map/ppermute | solution.py:16
  419.2 8.2 %collective-permute-start.6 = (bf16[512,128]{1,0:T(8,128)(2,1)S(1)}, bf16[512,128]{1,0:T(8,128)(2,1)S(1)}, u32[]{:S(2)}, u32[]{:S(2)}) collective-permute-start(bf16[512,128]{1,0:T(8,128)(2,1)S(1)} %collective-permute-done.5), channel_id=1, source_target_pairs={{0,128},{8,136},{16,144},{24,152},{32,160},{40,168},{48,176},{56,1... | collective-permute-start | bytes 393224 | tf_op jit(solution)/shard_map/ppermute | solution.py:16
  427.4 8.4 %collective-permute-start.7 = (bf16[512,128]{1,0:T(8,128)(2,1)S(1)}, bf16[512,128]{1,0:T(8,128)(2,1)S(1)}, u32[]{:S(2)}, u32[]{:S(2)}) collective-permute-start(bf16[512,128]{1,0:T(8,128)(2,1)S(1)} %collective-permute-done.6), channel_id=1, source_target_pairs={{0,256},{8,264},{16,272},{24,280},{32,288},{40,296},{48,304},{56,3... | collective-permute-start | bytes 393224 | tf_op jit(solution)/shard_map/ppermute | solution.py:16
Sparse Core Ops, SparseCore 0:
  46.9 83.4 all-reduce.1
  133.4 45.2 reduce-scatter.3
  186.6 42.5 all-gather.1
where the time goes:
time: 445 us; the launch traced here: 444 us
  waiting for transfers between devices  327 us (73%)
  starting transfers between devices  36.2 us (8%)
  blocking collectives  32.5 us (7%)
  between operations  14 us (3%)
  local copies, waits for them, and re-layouts  13 us (3%)
  other arithmetic  11.7 us (3%)
  matrix products  10 us (2%)
    ppermute x6, waiting for transfers between devices, from_partner(): lax.ppermute(x, axis, [(i, i ^ 1 << apart) for i in range(lax.axis_size(a...  133 us
    psum x1, waiting for transfers between devices, shards(): lax.psum(jnp.dot(columns, keyval_weight, preferred_element_type=jnp.float...  76.9 us
    unnamed x4, waiting for transfers between devices  47.3 us
    all_gather x1, waiting for transfers between devices, shards(): lax.all_gather(head_out, 'seq', axis=1, tiled=True)  42.7 us
    all_to_all x1, blocking collectives, shards(): lax.all_to_all(normed, 'seq', split_axis=1, concat_axis=0, tiled=True)  32.5 us
    all_to_all x1, waiting for transfers between devices, shards(): lax.all_to_all(attn_cols.astype(jnp.bfloat16), 'seq', split_axis=0, conca...  26.6 us
    ppermute x6, starting transfers between devices, from_partner(): lax.ppermute(x, axis, [(i, i ^ 1 << apart) for i in range(lax.axis_size(a...  21.8 us
    ppermute x2, starting transfers between devices, from_behind(): return lax.ppermute(x, axis, pairs)  10.6 us
  transfers between devices with their start and end apart: 12, of which 10 were waited for; matrix products, arithmetic and copies ran while one was open for 2% of the time, Pallas kernels for 0%

commit v1 on v0

v1 whole, which is shorter than its diff:
```python
import math

import jax
import jax.numpy as jnp
from jax import lax
from jax.experimental import pallas as pl
from jax.experimental.pallas import tpu as pltpu
from jax.sharding import PartitionSpec as P

VMEM_LIMIT = 40 * 1024 * 1024


def exchange(x, flip):
    size = lax.axis_size("seq")
    return lax.ppermute(x, "seq", [(i, i ^ flip) for i in range(size)])


def across(x, flip):
    sections, size = lax.axis_size("section"), lax.axis_size("seq")
    pairs = [
        (s * size + i, (s ^ 1) * size + (i ^ flip)) for s in range(sections) for i in range(size)
    ]
    return lax.ppermute(x, ("section", "seq"), pairs)


def piece(place, k):
    return (place % 4) ^ (2 * (k // 2) + k % 2)


def call(kernel, outs, *args):
    return pl.pallas_call(
        kernel,
        out_shape=outs,
        in_specs=[pl.BlockSpec(memory_space=pltpu.SMEM)]
        + [pl.BlockSpec(memory_space=pltpu.VMEM)] * (len(args) - 1),
        compiler_params=pltpu.CompilerParams(vmem_limit_bytes=VMEM_LIMIT),
    )(*args)


def project_kernel(place_ref, own_ref, far_ref, gain_ref, w0, w1, w2, w3, near_out, far_out):
    place = place_ref[0]
    half = place // 4
    near = None
    far = None
    width = w0.shape[0]
    for k, weight in enumerate((w0, w1, w2, w3)):
        part = piece(place, k)
        start = pl.multiple_of(part * width, width)
        whole = pl.multiple_of((half * 4 + part) * width, width)
        gain = gain_ref[:, pl.ds(whole, width)]
        a = (own_ref[:, pl.ds(whole, width)].astype(jnp.float32) * gain).astype(jnp.bfloat16)
        b = (far_ref[:, pl.ds(start, width)].astype(jnp.float32) * gain).astype(jnp.bfloat16)
        w = weight[...]
        a = jnp.dot(a, w, preferred_element_type=jnp.float32)
        b = jnp.dot(b, w, preferred_element_type=jnp.float32)
        near = a if near is None else near + a
        far = b if far is None else far + b
    near_out[...] = near
    far_out[...] = far.astype(jnp.bfloat16)


def rope(values, cosine, sine):
    return values * cosine + pltpu.roll(values, values.shape[1] // 2, axis=1) * sine


def keyval_kernel(near_ref, far_ref, scale_ref, cos_ref, sin_ref, out_ref):
    total = (near_ref[...] + far_ref[...].astype(jnp.float32)) * scale_ref[...]
    size = total.shape[1] // 2
    out_ref[:, :size] = rope(total[:, :size], cos_ref[...], sin_ref[...]).astype(jnp.bfloat16)
    out_ref[:, size:] = total[:, size:].astype(jnp.bfloat16)


def attend_kernel(place_ref, near_ref, far_ref, scale_ref, cos_ref, sin_ref, kv_ref, out_ref):
    rows, width = near_ref.shape
    length = kv_ref.shape[0]
    size = kv_ref.shape[1] // 2
    keys = kv_ref[:, :size]
    values = kv_ref[:, size:]
    row_ids = place_ref[0] * rows + lax.broadcasted_iota(jnp.int32, (rows, length), 0)
    keep = lax.broadcasted_iota(jnp.int32, (rows, length), 1) <= row_ids
    scale = scale_ref[...]
    cosine = cos_ref[...]
    sine = sin_ref[...]
    for head in range(width // size):
        cols = slice(head * size, (head + 1) * size)
        total = (near_ref[:, cols] + far_ref[:, cols].astype(jnp.float32)) * scale
        query = rope(total, cosine, sine).astype(jnp.bfloat16)
        scores = lax.dot_general(
            query, keys, (((1,), (1,)), ((), ())), preferred_element_type=jnp.float32
        ) * (1.0 / math.sqrt(size))
        scores = jnp.where(keep, scores, jnp.float32(-1e30))
        raised = jnp.exp(scores - jnp.max(scores, axis=1, keepdims=True))
        total = jnp.sum(raised, axis=1, keepdims=True)
        mixed = jnp.dot(raised.astype(jnp.bfloat16), values, preferred_element_type=jnp.float32)
        out_ref[:, cols] = (mixed / total).astype(jnp.bfloat16)


def output_kernel(
    place_ref, heads_ref, far_heads_ref, own_ref, far_ref, w0, w1, w2, w3, near_out, far_out
):
    place = place_ref[0]
    half = place // 4
    width = w0.shape[1]
    near = heads_ref[...]
    far = far_heads_ref[...]
    for k, weight in enumerate((w0, w1, w2, w3)):
        part = piece(place, k)
        start = pl.multiple_of(part * width, width)
        whole = pl.multiple_of((half * 4 + part) * width, width)
        w = weight[...]
        a = jnp.dot(near, w, preferred_element_type=jnp.float32)
        b = jnp.dot(far, w, preferred_element_type=jnp.float32)
        a = a + own_ref[:, pl.ds(whole, width)].astype(jnp.float32)
        b = b + far_ref[:, pl.ds(start, width)].astype(jnp.float32)
        near_out[:, pl.ds(start, width)] = a.astype(jnp.bfloat16)
        far_out[:, pl.ds(start, width)] = b.astype(jnp.bfloat16)


def gathered(own):
    second = exchange(own, 2)
    return own, exchange(own, 1), second, exchange(second, 1)


def shards(section_input, norm_gain, w_query, w_keyval, w_out, down_grads, up_grads):
    rows = section_input[0]
    tokens, features = rows.shape
    seq = lax.axis_index("seq")
    half = seq // 4
    place = seq.astype(jnp.int32)[None]
    far_rows = exchange(
        lax.dynamic_slice_in_dim(rows, (1 - half) * (features // 2), features // 2, axis=1), 4
    )
    keyval_weights = gathered(w_keyval[0])
    query_weights = gathered(w_query[0])
    output_weights = gathered(w_out[0])
    widened = rows.astype(jnp.float32)
    scale = lax.rsqrt(jnp.mean(widened * widened, axis=1, keepdims=True) + 1e-05)
    size = w_keyval.shape[2] // 2
    frequency = 10000.0 ** (-(jnp.arange(size // 2, dtype=jnp.float32) * 2.0 / size))
    positions = (seq * tokens + jnp.arange(tokens)).astype(jnp.float32)
    angles = positions[:, None] * frequency[None, :]
    cosine = jnp.cos(angles)
    sine = jnp.sin(angles)
    cosine = jnp.concatenate([cosine, cosine], axis=1)
    sine = jnp.concatenate([-sine, sine], axis=1)

    def partials(weights):
        width = weights[0].shape[1]
        outs = (
            jax.ShapeDtypeStruct((tokens, width), jnp.float32),
            jax.ShapeDtypeStruct((tokens, width), jnp.bfloat16),
        )
        return call(project_kernel, outs, place, rows, far_rows, norm_gain, *weights)

    near, far = partials(keyval_weights)
    keyval = pl.pallas_call(
        keyval_kernel, out_shape=jax.ShapeDtypeStruct((tokens, 2 * size), jnp.bfloat16)
    )(near, exchange(far, 4), scale, cosine, sine)
    keyval = lax.all_gather(keyval, "seq", axis=0, tiled=True)
    near, far = partials(query_weights)
    heads = call(
        attend_kernel,
        jax.ShapeDtypeStruct(near.shape, jnp.bfloat16),
        place, near, exchange(far, 4), scale, cosine, sine, keyval,
    )
    out = jax.ShapeDtypeStruct((tokens, features // 2), jnp.bfloat16)
    near, far = call(
        output_kernel, (out, out), place, heads, exchange(heads, 4), rows, far_rows, *output_weights
    )
    near = across(near, 0)
    far = across(far, 4)
    first = half == 0
    received = jnp.concatenate(
        [jnp.where(first, near, far), jnp.where(first, far, near)], axis=1
    )
    sections = lax.axis_size("section")
    mirrored = lax.ppermute(up_grads[0], "section", [(i, sections - 1 - i) for i in range(sections)])
    grad_total = (down_grads[0].astype(jnp.float32) + mirrored.astype(jnp.float32)).astype(
        jnp.bfloat16
    )
    return (received[None], grad_total[None])


def solution(mesh):
    return jax.shard_map(
        shards,
        mesh=mesh,
        in_specs=(
            P("section", "seq", None),
            P("section", None),
            P("section", "seq", None),
            P("section", "seq", None),
            P("section", None, "seq"),
            P("section", "seq", None),
            P("section", "seq", None),
        ),
        out_specs=(P("section", "seq", None), P("section", "seq", None)),
        check_vma=False,
    )
```

time: 445 us -> 236 us (0.53)
  the two profiles are of different devices: /device:TPU:22 before, /device:TPU:71 now
where the time goes in v1:
time: 236 us
  waiting for transfers between devices  132 us (56%)
  starting transfers between devices  63.7 us (27%)
  blocking collectives  17.6 us (7%)
  Pallas kernels  13.9 us (6%)
  local copies, waits for them, and re-layouts  4.22 us (2%)
  other arithmetic  3.21 us (1%)
    ppermute x2, waiting for transfers between devices, across(): return lax.ppermute(x, ('section', 'seq'), pairs)  60.2 us
    ppermute x13, waiting for transfers between devices, exchange(): return lax.ppermute(x, 'seq', [(i, i ^ flip) for i in range(size)])  57.7 us
    ppermute x13, starting transfers between devices, exchange(): return lax.ppermute(x, 'seq', [(i, i ^ flip) for i in range(size)])  38.6 us
    all_gather x1, blocking collectives, shards(): keyval = lax.all_gather(keyval, 'seq', axis=0, tiled=True)  17.6 us
    ppermute x1, waiting for transfers between devices, shards(): lax.ppermute(up_grads[0], 'section', [(i, sections - 1 - i) for i in rang...  14 us
    ppermute x1, starting transfers between devices, shards(): lax.ppermute(up_grads[0], 'section', [(i, sections - 1 - i) for i in rang...  13.3 us
    pallas_call x4, Pallas kernels, call(): pl.pallas_call(kernel, out_shape=outs, in_specs=[pl.BlockSpec(memory_spac...  12.1 us
    ppermute x2, starting transfers between devices, across(): return lax.ppermute(x, ('section', 'seq'), pairs)  11.8 us
  transfers between devices with their start and end apart: 16, of which 8 were waited for; matrix products, arithmetic and copies ran while one was open for 2% of the time, Pallas kernels for 4%

profile of v1, /device:TPU:71, one launch (start us, length us, event | category | flops | bytes accessed | tf_op | source)
XLA Modules:
  0.0 235.5 jit_solution(9258527651778617595)
XLA Ops:
  0.6 3.7 %collective-permute-start.2 = (bf16[512,1024]{1,0:T(8,128)(2,1)}, bf16[512,1024]{1,0:T(8,128)(2,1)}, u32[]{:S(2)}, u32[]{:S(2)}) collective-permute-start(bf16[512,1024]{1,0:T(8,128)(2,1)} %bitcast.24), channel_id=1, source_target_pairs={{0,2},{1,3},{2,0},{3,1},{4,6},{5,7},{6,4},{7,5},{8,10},{9,11},{10,... | collective-permute-start | bytes 3145736 | tf_op jit(solution)/shard_map/ppermute | solution.py:15
  4.3 1.9 collective-permute-start.11
  6.3 3.4 %collective-permute-start.6 = (bf16[512,256]{1,0:T(8,128)(2,1)}, bf16[512,256]{1,0:T(8,128)(2,1)S(1)}, u32[]{:S(2)}, u32[]{:S(2)}) collective-permute-start(bf16[512,256]{1,0:T(8,128)(2,1)} %bitcast.27), channel_id=1, source_target_pairs={{0,2},{1,3},{2,0},{3,1},{4,6},{5,7},{6,4},{7,5},{8,10},{9,11},{10,... | collective-permute-start | bytes 786440 | tf_op jit(solution)/shard_map/ppermute | solution.py:15
  9.6 3.4 %collective-permute-start.1 = (bf16[512,1024]{1,0:T(8,128)(2,1)}, bf16[512,1024]{1,0:T(8,128)(2,1)}, u32[]{:S(2)}, u32[]{:S(2)}) collective-permute-start(bf16[512,1024]{1,0:T(8,128)(2,1)} %bitcast.25), channel_id=1, source_target_pairs={{0,1},{1,0},{2,3},{3,2},{4,5},{5,4},{6,7},{7,6},{8,9},{9,8},{10,11... | collective-permute-start | bytes 3145736 | tf_op jit(solution)/shard_map/ppermute | solution.py:15
  13.1 14.3 %collective-permute-done.2.w2 = bf16[512,1024]{1,0:T(8,128)(2,1)} collective-permute-done((bf16[512,1024]{1,0:T(8,128)(2,1)}, bf16[512,1024]{1,0:T(8,128)(2,1)}, u32[]{:S(2)}, u32[]{:S(2)}) %collective-permute-start.2) | collective-permute-done | bytes 1048608 | tf_op jit(solution)/shard_map/ppermute | solution.py:15
  27.4 4.2 %collective-permute-start.3 = (bf16[512,1024]{1,0:T(8,128)(2,1)}, bf16[512,1024]{1,0:T(8,128)(2,1)}, u32[]{:S(2)}, u32[]{:S(2)}) collective-permute-start(bf16[512,1024]{1,0:T(8,128)(2,1)} %collective-permute-done.2.w2), channel_id=1, source_target_pairs={{0,1},{1,0},{2,3},{3,2},{4,5},{5,4},{6,7},{7,6},{8,9},{9,8},{10,11... | collective-permute-start | bytes 3145736 | tf_op jit(solution)/shard_map/ppermute | solution.py:15
  31.6 1.9 dynamic-slice_bitcast_fusion
  33.5 1.9 collective-permute-start
  35.4 30.4 %collective-permute-done.6.w2 = bf16[512,256]{1,0:T(8,128)(2,1)S(1)} collective-permute-done((bf16[512,256]{1,0:T(8,128)(2,1)}, bf16[512,256]{1,0:T(8,128)(2,1)S(1)}, u32[]{:S(2)}, u32[]{:S(2)}) %collective-permute-start.6) | collective-permute-done | bytes 262176 | tf_op jit(solution)/shard_map/ppermute | solution.py:15
  65.8 3.4 %collective-permute-start.5 = (bf16[512,256]{1,0:T(8,128)(2,1)}, bf16[512,256]{1,0:T(8,128)(2,1)S(1)}, u32[]{:S(2)}, u32[]{:S(2)}) collective-permute-start(bf16[512,256]{1,0:T(8,128)(2,1)} %bitcast.28), channel_id=1, source_target_pairs={{0,1},{1,0},{2,3},{3,2},{4,5},{5,4},{6,7},{7,6},{8,9},{9,8},{10,11... | collective-permute-start | bytes 786440 | tf_op jit(solution)/shard_map/ppermute | solution.py:15
  69.5 1.0 collective-permute-done.5.w1
  70.6 2.3 collective-permute-start.10
  72.9 2.0 collective-permute-start.12
  74.9 2.3 collective-permute-start.7
  77.6 0.8 collective-permute-done.7.w3
  78.4 0.9 copy-done.6
  79.8 1.9 collective-permute-start.8
  81.8 3.8 %shard_map.86 = (f32[128,1024]{1,0:T(8,128)S(1)}, bf16[128,1024]{1,0:T(8,128)(2,1)}) custom-call(s32[1]{0:T(128)} %bitcast.place_ref, bf16[128,4096]{1,0:T(8,128)(2,1)S(1)} %bitcast.19, bf16[128,2048]{1,0:T(8,128)(2,1)S(1)} %collective-permute-done.far_ref, f32[1,4096]{1,0:T(1,128)S(1)} %copy-done.8, bf16[512,1024]{1,0:T(8,128)(2,1)S(1)} %bitcast.26, ...), custom_call_target="tpu_custom_call" | custom-call | tf_op jit(solution)/shard_map/pallas_call | solution.py:31
  85.6 4.3 %collective-permute-start.4 = (bf16[128,1024]{1,0:T(8,128)(2,1)}, bf16[128,1024]{1,0:T(8,128)(2,1)}, u32[]{:S(2)}, u32[]{:S(2)}) collective-permute-start(bf16[128,1024]{1,0:T(8,128)(2,1)} %get-tuple-element.9), channel_id=1, source_target_pairs={{0,4},{1,5},{2,6},{3,7},{4,0},{5,1},{6,2},{7,3},{8,12},{9,13},{10,... | collective-permute-start | bytes 786440 | tf_op jit(solution)/shard_map/ppermute | solution.py:15
  92.0 1.8 shard_map.88
  93.8 17.6 %all_gather.3.kv_ref = bf16[1024,256]{1,0:T(8,128)(2,1)S(1)} all-gather(bf16[128,256]{1,0:T(8,128)(2,1)} %shard_map.88), channel_id=1, replica_groups=mesh['section'=64,'seq'=8] {'seq'}, dimensions={0}, use_global_device_ids=true | all-gather | bytes 589824 | tf_op jit(solution)/shard_map/all_gather | solution.py:159
  111.4 4.0 %shard_map.89.heads_ref = bf16[128,1024]{1,0:T(8,128)(2,1)S(1)} custom-call(s32[1]{0:T(128)} %bitcast.place_ref, f32[128,1024]{1,0:T(8,128)S(1)} %get-tuple-element.8.near_ref, bf16[128,1024]{1,0:T(8,128)(2,1)} %collective-permute-done.4.far_ref, f32[128,1]{1,0:T(8,128)S(1)} %copy-done.5, f32[128,128]{1,0:T(8,128)S(1)} %copy-done.3, ...), custom_call_target="tpu_custom_call" | custom-call | tf_op jit(solution)/shard_map/pallas_call | solution.py:31
  115.5 3.9 %collective-permute-start.9 = (bf16[128,1024]{1,0:T(8,128)(2,1)S(1)}, bf16[128,1024]{1,0:T(8,128)(2,1)S(1)}, u32[]{:S(2)}, u32[]{:S(2)}) collective-permute-start(bf16[128,1024]{1,0:T(8,128)(2,1)S(1)} %shard_map.89.heads_ref), channel_id=1, source_target_pairs={{0,4},{1,5},{2,6},{3,7},{4,0},{5,1},{6,2},{7,3},{8,12},{9,13},{10,... | collective-permute-start | bytes 786440 | tf_op jit(solution)/shard_map/ppermute | solution.py:15
  119.4 11.1 %collective-permute-done.9.far_heads_ref = bf16[128,1024]{1,0:T(8,128)(2,1)S(1)} collective-permute-done((bf16[128,1024]{1,0:T(8,128)(2,1)S(1)}, bf16[128,1024]{1,0:T(8,128)(2,1)S(1)}, u32[]{:S(2)}, u32[]{:S(2)}) %collective-permute-start.9) | collective-permute-done | bytes 262176 | tf_op jit(solution)/shard_map/ppermute | solution.py:15
  130.5 3.8 %shard_map.90 = (bf16[128,2048]{1,0:T(8,128)(2,1)}, bf16[128,2048]{1,0:T(8,128)(2,1)S(1)}) custom-call(s32[1]{0:T(128)} %bitcast.place_ref, bf16[128,1024]{1,0:T(8,128)(2,1)S(1)} %shard_map.89.heads_ref, bf16[128,1024]{1,0:T(8,128)(2,1)S(1)} %collective-permute-done.9.far_heads_ref, bf16[128,4096]{1,0:T(8,128)(2,1)S(1)} %bitcast.20, ...), custom_call_target="tpu_custom_call" | custom-call | tf_op jit(solution)/shard_map/pallas_call | solution.py:31
  134.3 8.8 %collective-permute-start.13 = (bf16[128,2048]{1,0:T(8,128)(2,1)}, bf16[128,2048]{1,0:T(8,128)(2,1)S(1)}, u32[]{:S(2)}, u32[]{:S(2)}) collective-permute-start(bf16[128,2048]{1,0:T(8,128)(2,1)} %get-tuple-element.12), channel_id=1, source_target_pairs={{0,8},{1,9},{2,10},{3,11},{4,12},{5,13},{6,14},{7,15},{8,0},{9,1},... | collective-permute-start | bytes 1572872 | tf_op jit(solution)/shard_map/ppermute | solution.py:23
  143.1 2.9 %collective-permute-start.14 = (bf16[128,2048]{1,0:T(8,128)(2,1)S(1)}, bf16[128,2048]{1,0:T(8,128)(2,1)S(1)}, u32[]{:S(2)}, u32[]{:S(2)}) collective-permute-start(bf16[128,2048]{1,0:T(8,128)(2,1)S(1)} %get-tuple-element.13), channel_id=1, source_target_pairs={{0,12},{1,13},{2,14},{3,15},{4,8},{5,9},{6,10},{7,11},{8,4},{9,5},... | collective-permute-start | bytes 1572872 | tf_op jit(solution)/shard_map/ppermute | solution.py:23
  146.1 13.3 %collective-permute-start.15 = (bf16[512,128]{1,0:T(8,128)(2,1)S(1)}, bf16[512,128]{1,0:T(8,128)(2,1)S(1)}, u32[]{:S(2)}, u32[]{:S(2)}) collective-permute-start(bf16[512,128]{1,0:T(8,128)(2,1)S(1)} %bitcast.30), channel_id=1, source_target_pairs={{0,504},{8,496},{16,488},{24,480},{32,472},{40,464},{48,456},{56,4... | collective-permute-start | bytes 393224 | tf_op jit(solution)/shard_map/ppermute | solution.py:177
  159.5 14.0 %collective-permute-done.15 = bf16[512,128]{1,0:T(8,128)(2,1)S(1)} collective-permute-done((bf16[512,128]{1,0:T(8,128)(2,1)S(1)}, bf16[512,128]{1,0:T(8,128)(2,1)S(1)}, u32[]{:S(2)}, u32[]{:S(2)}) %collective-permute-start.15) | collective-permute-done | bytes 131104 | tf_op jit(solution)/shard_map/ppermute | solution.py:177
  174.2 27.9 %collective-permute-done.13 = bf16[128,2048]{1,0:T(8,128)(2,1)S(1)} collective-permute-done((bf16[128,2048]{1,0:T(8,128)(2,1)}, bf16[128,2048]{1,0:T(8,128)(2,1)S(1)}, u32[]{:S(2)}, u32[]{:S(2)}) %collective-permute-start.13) | collective-permute-done | bytes 524320 | tf_op jit(solution)/shard_map/ppermute | solution.py:23
  202.1 32.3 %collective-permute-done.14 = bf16[128,2048]{1,0:T(8,128)(2,1)S(1)} collective-permute-done((bf16[128,2048]{1,0:T(8,128)(2,1)S(1)}, bf16[128,2048]{1,0:T(8,128)(2,1)S(1)}, u32[]{:S(2)}, u32[]{:S(2)}) %collective-permute-start.14) | collective-permute-done | bytes 524320 | tf_op jit(solution)/shard_map/ppermute | solution.py:23
  234.5 1.1 maximum_bitcast_fusion
  (41 shorter events, 4.0 us)
Async XLA Ops:
  0.6 68.6 %copy-start = (bf16[1,128,4096]{2,1,0:T(8,128)(2,1)S(1)}, bf16[1,128,4096]{2,1,0:T(8,128)(2,1)}, u32[]{:S(2)}) copy-start(bf16[1,128,4096]{2,1,0:T(8,128)(2,1)} %param.7) | copy-start | bytes 3145732
  0.6 26.8 %collective-permute-start.2 = (bf16[512,1024]{1,0:T(8,128)(2,1)}, bf16[512,1024]{1,0:T(8,128)(2,1)}, u32[]{:S(2)}, u32[]{:S(2)}) collective-permute-start(bf16[512,1024]{1,0:T(8,128)(2,1)} %bitcast.24), channel_id=1, source_target_pairs={{0,2},{1,3},{2,0},{3,1},{4,6},{5,7},{6,4},{7,5},{8,10},{9,11},{10,... | collective-permute-start | bytes 3145736 | tf_op jit(solution)/shard_map/ppermute | solution.py:15
  4.3 68.5 %collective-permute-start.11 = (bf16[1024,512]{1,0:T(8,128)(2,1)}, bf16[1024,512]{1,0:T(8,128)(2,1)}, u32[]{:S(2)}, u32[]{:S(2)}) collective-permute-start(bf16[1024,512]{1,0:T(8,128)(2,1)} %bitcast.21), channel_id=1, source_target_pairs={{0,2},{1,3},{2,0},{3,1},{4,6},{5,7},{6,4},{7,5},{8,10},{9,11},{10,... | collective-permute-start | bytes 3145736 | tf_op jit(solution)/shard_map/ppermute | solution.py:15
  6.3 59.5 %collective-permute-start.6 = (bf16[512,256]{1,0:T(8,128)(2,1)}, bf16[512,256]{1,0:T(8,128)(2,1)S(1)}, u32[]{:S(2)}, u32[]{:S(2)}) collective-permute-start(bf16[512,256]{1,0:T(8,128)(2,1)} %bitcast.27), channel_id=1, source_target_pairs={{0,2},{1,3},{2,0},{3,1},{4,6},{5,7},{6,4},{7,5},{8,10},{9,11},{10,... | collective-permute-start | bytes 786440 | tf_op jit(solution)/shard_map/ppermute | solution.py:15
  9.6 72.1 %collective-permute-start.1 = (bf16[512,1024]{1,0:T(8,128)(2,1)}, bf16[512,1024]{1,0:T(8,128)(2,1)}, u32[]{:S(2)}, u32[]{:S(2)}) collective-permute-start(bf16[512,1024]{1,0:T(8,128)(2,1)} %bitcast.25), channel_id=1, source_target_pairs={{0,1},{1,0},{2,3},{3,2},{4,5},{5,4},{6,7},{7,6},{8,9},{9,8},{10,11... | collective-permute-start | bytes 3145736 | tf_op jit(solution)/shard_map/ppermute | solution.py:15
  13.1 57.5 %copy-start.1 = (bf16[1,1024,512]{2,1,0:T(8,128)(2,1)S(1)}, bf16[1,1024,512]{2,1,0:T(8,128)(2,1)}, u32[]{:S(2)}) copy-start(bf16[1,1024,512]{2,1,0:T(8,128)(2,1)} %param.11) | copy-start | bytes 3145732
  13.1 65.3 %copy-start.8 = (f32[1,4096]{1,0:T(1,128)S(1)}, f32[1,4096]{1,0:T(1,128)}, u32[]{:S(2)}) copy-start(f32[1,4096]{1,0:T(1,128)} %gain_ref.3) | copy-start | bytes 49156
  27.4 54.3 %collective-permute-start.3 = (bf16[512,1024]{1,0:T(8,128)(2,1)}, bf16[512,1024]{1,0:T(8,128)(2,1)}, u32[]{:S(2)}, u32[]{:S(2)}) collective-permute-start(bf16[512,1024]{1,0:T(8,128)(2,1)} %collective-permute-done.2.w2), channel_id=1, source_target_pairs={{0,1},{1,0},{2,3},{3,2},{4,5},{5,4},{6,7},{7,6},{8,9},{9,8},{10,11... | collective-permute-start | bytes 3145736 | tf_op jit(solution)/shard_map/ppermute | solution.py:15
  33.5 41.5 %collective-permute-start = (bf16[128,2048]{1,0:T(8,128)(2,1)}, bf16[128,2048]{1,0:T(8,128)(2,1)S(1)}, u32[]{:S(2)}, u32[]{:S(2)}) collective-permute-start(bf16[128,2048]{1,0:T(8,128)(2,1)} %dynamic-slice_bitcast_fusion), channel_id=1, source_target_pairs={{0,4},{1,5},{2,6},{3,7},{4,0},{5,1},{6,2},{7,3},{8,12},{9,13},{10,... | collective-permute-start | bytes 1572872 | tf_op jit(solution)/shard_map/ppermute | solution.py:15
  65.8 4.8 %collective-permute-start.5 = (bf16[512,256]{1,0:T(8,128)(2,1)}, bf16[512,256]{1,0:T(8,128)(2,1)S(1)}, u32[]{:S(2)}, u32[]{:S(2)}) collective-permute-start(bf16[512,256]{1,0:T(8,128)(2,1)} %bitcast.28), channel_id=1, source_target_pairs={{0,1},{1,0},{2,3},{3,2},{4,5},{5,4},{6,7},{7,6},{8,9},{9,8},{10,11... | collective-permute-start | bytes 786440 | tf_op jit(solution)/shard_map/ppermute | solution.py:15
  70.6 48.8 %collective-permute-start.10 = (bf16[1024,512]{1,0:T(8,128)(2,1)S(1)}, bf16[1024,512]{1,0:T(8,128)(2,1)}, u32[]{:S(2)}, u32[]{:S(2)}) collective-permute-start(bf16[1024,512]{1,0:T(8,128)(2,1)S(1)} %bitcast.22), channel_id=1, source_target_pairs={{0,1},{1,0},{2,3},{3,2},{4,5},{5,4},{6,7},{7,6},{8,9},{9,8},{10,11... | collective-permute-start | bytes 3145736 | tf_op jit(solution)/shard_map/ppermute | solution.py:15
  72.9 46.5 %collective-permute-start.12 = (bf16[1024,512]{1,0:T(8,128)(2,1)}, bf16[1024,512]{1,0:T(8,128)(2,1)}, u32[]{:S(2)}, u32[]{:S(2)}) collective-permute-start(bf16[1024,512]{1,0:T(8,128)(2,1)} %collective-permute-done.11.w2), channel_id=1, source_target_pairs={{0,1},{1,0},{2,3},{3,2},{4,5},{5,4},{6,7},{7,6},{8,9},{9,8},{10,11... | collective-permute-start | bytes 3145736 | tf_op jit(solution)/shard_map/ppermute | solution.py:15
  74.9 3.4 %collective-permute-start.7 = (bf16[512,256]{1,0:T(8,128)(2,1)S(1)}, bf16[512,256]{1,0:T(8,128)(2,1)S(1)}, u32[]{:S(2)}, u32[]{:S(2)}) collective-permute-start(bf16[512,256]{1,0:T(8,128)(2,1)S(1)} %collective-permute-done.6.w2), channel_id=1, source_target_pairs={{0,1},{1,0},{2,3},{3,2},{4,5},{5,4},{6,7},{7,6},{8,9},{9,8},{10,11... | collective-permute-start | bytes 786440 | tf_op jit(solution)/shard_map/ppermute | solution.py:15
  78.4 1.0 copy-start.6
  79.3 2.4 %copy-start.2 = (bf16[1,512,1024]{2,1,0:T(8,128)(2,1)S(1)}, bf16[1,512,1024]{2,1,0:T(8,128)(2,1)}, u32[]{:S(2)}) copy-start(bf16[1,512,1024]{2,1,0:T(8,128)(2,1)} %param.9) | copy-start | bytes 3145732
  79.8 5.8 %copy-start.7 = (f32[128,256]{1,0:T(8,128)}, f32[128,256]{1,0:T(8,128)S(1)}, u32[]{:S(2)}) copy-start(f32[128,256]{1,0:T(8,128)S(1)} %get-tuple-element.10.near_ref) | copy-start | bytes 393220
  79.8 11.6 %collective-permute-start.8 = (bf16[128,256]{1,0:T(8,128)(2,1)S(1)}, bf16[128,256]{1,0:T(8,128)(2,1)S(1)}, u32[]{:S(2)}, u32[]{:S(2)}) collective-permute-start(bf16[128,256]{1,0:T(8,128)(2,1)S(1)} %get-tuple-element.11), channel_id=1, source_target_pairs={{0,4},{1,5},{2,6},{3,7},{4,0},{5,1},{6,2},{7,3},{8,12},{9,13},{10,... | collective-permute-start | bytes 196616 | tf_op jit(solution)/shard_map/ppermute | solution.py:15
  85.6 25.8 %collective-permute-start.4 = (bf16[128,1024]{1,0:T(8,128)(2,1)}, bf16[128,1024]{1,0:T(8,128)(2,1)}, u32[]{:S(2)}, u32[]{:S(2)}) collective-permute-start(bf16[128,1024]{1,0:T(8,128)(2,1)} %get-tuple-element.9), channel_id=1, source_target_pairs={{0,4},{1,5},{2,6},{3,7},{4,0},{5,1},{6,2},{7,3},{8,12},{9,13},{10,... | collective-permute-start | bytes 786440 | tf_op jit(solution)/shard_map/ppermute | solution.py:15
  90.6 20.8 %copy-start.3 = (f32[128,128]{1,0:T(8,128)S(1)}, f32[128,128]{1,0:T(8,128)}, u32[]{:S(2)}) copy-start(f32[128,128]{1,0:T(8,128)} %get-tuple-element.19.cos_ref) | copy-start | bytes 196612
  90.6 20.8 %copy-start.4 = (f32[128,128]{1,0:T(8,128)S(1)}, f32[128,128]{1,0:T(8,128)}, u32[]{:S(2)}) copy-start(f32[128,128]{1,0:T(8,128)} %get-tuple-element.20.sin_ref) | copy-start | bytes 196612
  91.4 20.0 %copy-start.5 = (f32[128,1]{1,0:T(8,128)S(1)}, f32[128,1]{1,0:T(8,128)}, u32[]{:S(2)}) copy-start(f32[128,1]{1,0:T(8,128)} %copy.10.scale_ref) | copy-start | bytes 1540
  91.4 0.6 copy-start.10
  115.5 30.6 %copy-start.11 = (bf16[1,512,128]{2,1,0:T(8,128)(2,1)S(1)}, bf16[1,512,128]{2,1,0:T(8,128)(2,1)}, u32[]{:S(2)}) copy-start(bf16[1,512,128]{2,1,0:T(8,128)(2,1)} %param.13) | copy-start | bytes 393220
  115.5 58.0 %copy-start.9 = (bf16[1,512,128]{2,1,0:T(8,128)(2,1)S(1)}, bf16[1,512,128]{2,1,0:T(8,128)(2,1)}, u32[]{:S(2)}) copy-start(bf16[1,512,128]{2,1,0:T(8,128)(2,1)} %param.12) | copy-start | bytes 393220
  115.5 15.0 %collective-permute-start.9 = (bf16[128,1024]{1,0:T(8,128)(2,1)S(1)}, bf16[128,1024]{1,0:T(8,128)(2,1)S(1)}, u32[]{:S(2)}, u32[]{:S(2)}) collective-permute-start(bf16[128,1024]{1,0:T(8,128)(2,1)S(1)} %shard_map.89.heads_ref), channel_id=1, source_target_pairs={{0,4},{1,5},{2,6},{3,7},{4,0},{5,1},{6,2},{7,3},{8,12},{9,13},{10,... | collective-permute-start | bytes 786440 | tf_op jit(solution)/shard_map/ppermute | solution.py:15
  134.3 67.8 %collective-permute-start.13 = (bf16[128,2048]{1,0:T(8,128)(2,1)}, bf16[128,2048]{1,0:T(8,128)(2,1)S(1)}, u32[]{:S(2)}, u32[]{:S(2)}) collective-permute-start(bf16[128,2048]{1,0:T(8,128)(2,1)} %get-tuple-element.12), channel_id=1, source_target_pairs={{0,8},{1,9},{2,10},{3,11},{4,12},{5,13},{6,14},{7,15},{8,0},{9,1},... | collective-permute-start | bytes 1572872 | tf_op jit(solution)/shard_map/ppermute | solution.py:23
  143.1 91.2 %collective-permute-start.14 = (bf16[128,2048]{1,0:T(8,128)(2,1)S(1)}, bf16[128,2048]{1,0:T(8,128)(2,1)S(1)}, u32[]{:S(2)}, u32[]{:S(2)}) collective-permute-start(bf16[128,2048]{1,0:T(8,128)(2,1)S(1)} %get-tuple-element.13), channel_id=1, source_target_pairs={{0,12},{1,13},{2,14},{3,15},{4,8},{5,9},{6,10},{7,11},{8,4},{9,5},... | collective-permute-start | bytes 1572872 | tf_op jit(solution)/shard_map/ppermute | solution.py:23
  146.1 27.4 %collective-permute-start.15 = (bf16[512,128]{1,0:T(8,128)(2,1)S(1)}, bf16[512,128]{1,0:T(8,128)(2,1)S(1)}, u32[]{:S(2)}, u32[]{:S(2)}) collective-permute-start(bf16[512,128]{1,0:T(8,128)(2,1)S(1)} %bitcast.30), channel_id=1, source_target_pairs={{0,504},{8,496},{16,488},{24,480},{32,472},{40,464},{48,456},{56,4... | collective-permute-start | bytes 393224 | tf_op jit(solution)/shard_map/ppermute | solution.py:177

commit v2 on v1

v2 whole, which is shorter than its diff:
```python
import math

import jax
import jax.numpy as jnp
from jax import lax
from jax.experimental import pallas as pl
from jax.experimental.pallas import tpu as pltpu
from jax.sharding import PartitionSpec as P

LEADING = 64
VMEM_LIMIT = 8 * 1024 * 1024


def exchange(x, flip):
    size = lax.axis_size("seq")
    return lax.ppermute(x, "seq", [(i, i ^ flip) for i in range(size)])


def across(x, flip):
    sections, size = lax.axis_size("section"), lax.axis_size("seq")
    pairs = [
        (s * size + i, (s ^ 1) * size + (i ^ flip)) for s in range(sections) for i in range(size)
    ]
    return lax.ppermute(x, ("section", "seq"), pairs)


def piece(place, k):
    return (place % 4) ^ (2 * (k // 2) + k % 2)


def after(x, *others):
    return lax.optimization_barrier((x,) + others)[0]


def call(kernel, outs, *args):
    return pl.pallas_call(
        kernel,
        out_shape=outs,
        in_specs=[pl.BlockSpec(memory_space=pltpu.SMEM)]
        + [pl.BlockSpec(memory_space=pltpu.VMEM)] * (len(args) - 1),
        compiler_params=pltpu.CompilerParams(vmem_limit_bytes=VMEM_LIMIT),
        cost_estimate=pl.CostEstimate(flops=1, transcendentals=0, bytes_accessed=1),
    )(*args)


def scale_kernel(place_ref, rows_ref, out_ref):
    rows = rows_ref[...].astype(jnp.float32)
    scale = lax.rsqrt(jnp.mean(rows * rows, axis=1, keepdims=True) + 1e-05)
    out_ref[...] = jnp.broadcast_to(scale, out_ref.shape)


def dot(a, b):
    return jnp.dot(a, b, preferred_element_type=jnp.float32)


def project(place, own_ref, far_ref, gain_ref, weights, pieces):
    half = place // 4
    near = None
    far = None
    for k, weight in zip(pieces, weights):
        width = weight.shape[0]
        part = piece(place, k)
        start = pl.multiple_of(part * width, width)
        whole = pl.multiple_of((half * 4 + part) * width, width)
        gain = gain_ref[:, pl.ds(whole, width)]
        a = (own_ref[:, pl.ds(whole, width)].astype(jnp.float32) * gain).astype(jnp.bfloat16)
        b = (far_ref[:, pl.ds(start, width)].astype(jnp.float32) * gain).astype(jnp.bfloat16)
        w = weight[...]
        total = dot(jnp.concatenate([a, b], axis=0), w)
        a, b = total[: a.shape[0]], total[a.shape[0] :]
        near = a if near is None else near + a
        far = b if far is None else far + b
    return near, far


def project_kernel(place_ref, own_ref, far_ref, gain_ref, w0, w1, w2, w3, near_out, far_out):
    near, far = project(
        place_ref[0], own_ref, far_ref, gain_ref, (w0, w1, w2, w3), (0, 1, 2, 3)
    )
    near_out[...] = near
    far_out[...] = far.astype(jnp.bfloat16)


def rope(values, cosine, sine):
    return values * cosine + pltpu.roll(values, values.shape[1] // 2, axis=1) * sine


def collect_kernel(place_ref, near_ref, far_ref, scale_ref, cos_ref, sin_ref, out_ref):
    total = near_ref[...] + far_ref[...].astype(jnp.float32)
    scale = scale_ref[...]
    size = total.shape[1] // 2
    keys = rope(total[:, :size] * scale, cos_ref[...], sin_ref[...]).astype(jnp.bfloat16)
    values = (total[:, size:] * scale).astype(jnp.bfloat16)
    for k in range(out_ref.shape[0]):
        out_ref[k, :, :size] = keys
        out_ref[k, :, size:] = values


def attend_kernel(
    place_ref, near_ref, far_ref, scale_ref, cos_ref, sin_ref, kv_ref, out_ref
):
    rows, width = near_ref.shape
    length = kv_ref.shape[0]
    size = kv_ref.shape[1] // 2
    keys = kv_ref[:, :size]
    values = kv_ref[:, size:]
    row_ids = place_ref[0] * rows
    row_ids = row_ids + lax.broadcasted_iota(jnp.int32, (rows, length), 0)
    keep = lax.broadcasted_iota(jnp.int32, (rows, length), 1) <= row_ids
    scale = scale_ref[...]
    cosine = cos_ref[...]
    sine = sin_ref[...]
    for head in range(width // size):
        cols = slice(head * size, (head + 1) * size)
        total = (near_ref[:, cols] + far_ref[:, cols].astype(jnp.float32)) * scale
        query = rope(total, cosine, sine).astype(jnp.bfloat16)
        scores = lax.dot_general(
            query, keys, (((1,), (1,)), ((), ())), preferred_element_type=jnp.float32
        ) * (1.0 / math.sqrt(size))
        scores = jnp.where(keep, scores, jnp.float32(-1e30))
        raised = jnp.exp(scores - jnp.max(scores, axis=1, keepdims=True))
        total = jnp.sum(raised, axis=1, keepdims=True)
        out_ref[:, cols] = (dot(raised.astype(jnp.bfloat16), values) / total).astype(jnp.bfloat16)


def output_kernel(far, place_ref, heads, rows_ref, *refs):
    weights, outs = refs[:4], refs[4:]
    place = place_ref[0]
    base = 0 if far else place // 4 * 4
    for k, weight in enumerate(weights):
        width = weight.shape[1]
        part = piece(place, k)
        start = pl.multiple_of(part * width, width)
        whole = pl.multiple_of((base + part) * width, width)
        total = dot(heads[...], weight[...])
        total = total + rows_ref[:, pl.ds(whole, width)].astype(jnp.float32)
        row = 0
        for out in outs:
            some = total[row : row + out.shape[0]]
            out[:, pl.ds(start, width)] = some.astype(jnp.bfloat16)
            row += out.shape[0]


def assemble_kernel(place_ref, first, second, far, out_ref):
    half = place_ref[0] // 4
    rows, width = first.shape
    near_cols = pl.ds(pl.multiple_of(half * width, width), width)
    out_ref[:rows, near_cols] = first[...]
    out_ref[rows:, near_cols] = second[...]
    out_ref[:, pl.ds(pl.multiple_of((1 - half) * width, width), width)] = far[...]


def at_row(kernel, *fixed):
    def run(*refs):
        kernel(*fixed, *refs)

    return run


def shards(section_input, norm_gain, w_query, w_keyval, w_out, down_grads, up_grads):
    rows = section_input[0]
    tokens, features = rows.shape
    size = w_keyval.shape[2] // 2
    wide = w_query.shape[2]
    bf16, f32 = jnp.bfloat16, jnp.float32
    seq = lax.axis_index("seq")
    half = seq // 4
    place = seq.astype(jnp.int32)[None]

    def array(count, columns, kind=bf16):
        return jax.ShapeDtypeStruct((count, columns), kind)

    sent = lax.dynamic_slice_in_dim(rows, (1 - half) * (features // 2), features // 2, axis=1)
    far_rows = exchange(sent, 4)
    keyval_2 = exchange(w_keyval[0], 2)
    keyval_1 = exchange(w_keyval[0], 1)
    scale = call(scale_kernel, array(tokens, size, f32), place, after(rows, sent))
    w_query = after(w_query[0], scale)
    query_2 = exchange(w_query, 2)
    query_1 = exchange(w_query, 1)
    keyval_3 = exchange(keyval_2, 1)
    query_3 = exchange(query_2, 1)
    out_1 = exchange(after(w_out[0], scale), 1)

    frequency = 10000.0 ** (-(jnp.arange(size // 2, dtype=f32) * 2.0 / size))
    positions = (seq * tokens + jnp.arange(tokens)).astype(f32)
    angles = positions[:, None] * frequency[None, :]
    cosine = jnp.cos(angles)
    sine = jnp.sin(angles)
    cosine = jnp.concatenate([cosine, cosine], axis=1)
    sine = jnp.concatenate([-sine, sine], axis=1)

    near, far = call(
        project_kernel,
        (array(tokens, 2 * size, f32), array(tokens, 2 * size)),
        place, rows, far_rows, norm_gain, w_keyval[0], keyval_1, keyval_2, keyval_3,
    )
    far = exchange(far, 4)
    query_near, query_far = call(
        project_kernel,
        (array(tokens, wide, f32), array(tokens, wide)),
        place, rows, far_rows, norm_gain, w_query, query_1, query_2, query_3,
    )
    keyval = call(
        collect_kernel,
        jax.ShapeDtypeStruct((lax.axis_size("seq"), tokens, 2 * size), bf16),
        place, near, far, scale, cosine, sine,
    )
    keyval = lax.all_to_all(keyval, "seq", split_axis=0, concat_axis=0, tiled=True)
    keyval = keyval.reshape(-1, 2 * size)
    query_far = exchange(query_far, 4)
    heads = call(
        attend_kernel,
        array(tokens, wide),
        place, query_near, query_far, scale, cosine, sine, keyval,
    )
    far_heads = exchange(heads, 4)
    out_2 = exchange(after(w_out[0], query_2), 2)
    out_3 = exchange(after(out_2, heads), 1)
    weights = w_out[0], out_1, out_2, out_3
    half_rows = array(tokens, features // 2)
    parts = tuple(array(n, features // 2) for n in (LEADING, tokens - LEADING))
    near = call(at_row(output_kernel, False), parts, place, heads, rows, *weights)
    far_heads = after(far_heads, *near)
    far = call(at_row(output_kernel, True), half_rows, place, far_heads, far_rows, *weights)
    first = across(near[0], 0)
    received = [first, across(after(near[1], first), 0), across(far, 4)]
    out = call(assemble_kernel, array(tokens, features), place, *received)
    sections = lax.axis_size("section")
    mirrored = lax.ppermute(
        after(up_grads[0], far),
        "section",
        [(i, sections - 1 - i) for i in range(sections)],
    )
    grad_total = (down_grads[0].astype(f32) + mirrored.astype(f32)).astype(bf16)
    return (out[None], grad_total[None])


def solution(mesh):
    return jax.shard_map(
        shards,
        mesh=mesh,
        in_specs=(
            P("section", "seq", None),
            P("section", None),
            P("section", "seq", None),
            P("section", "seq", None),
            P("section", None, "seq"),
            P("section", "seq", None),
            P("section", "seq", None),
        ),
        out_specs=(P("section", "seq", None), P("section", "seq", None)),
        check_vma=False,
    )
```

time: 236 us -> 205 us (0.87)
  the two profiles are of different devices: /device:TPU:71 before, /device:TPU:99 now
where the time goes in v2:
time: 205 us; the launch traced here: 204 us
  waiting for transfers between devices  103 us (50%)
  starting transfers between devices  81.5 us (40%)
  Pallas kernels  13.2 us (6%)
  local copies, waits for them, and re-layouts  4.59 us (2%)
    ppermute x3, waiting for transfers between devices, across(): return lax.ppermute(x, ('section', 'seq'), pairs)  53.7 us
    ppermute x13, waiting for transfers between devices, exchange(): return lax.ppermute(x, 'seq', [(i, i ^ flip) for i in range(size)])  48.9 us
    ppermute x13, starting transfers between devices, exchange(): return lax.ppermute(x, 'seq', [(i, i ^ flip) for i in range(size)])  33.5 us
    ppermute x3, starting transfers between devices, across(): return lax.ppermute(x, ('section', 'seq'), pairs)  23 us
    ppermute x1, starting transfers between devices, shards(): lax.ppermute(after(up_grads[0], far), 'section', [(i, sections - 1 - i) f...  17.9 us
    pallas_call x8, Pallas kernels, call(): pl.pallas_call(kernel, out_shape=outs, in_specs=[pl.BlockSpec(memory_spac...  13.2 us
    all_to_all x1, starting transfers between devices, shards(): lax.all_to_all(keyval, 'seq', split_axis=0, concat_axis=0, tiled=True)  7.09 us
  transfers between devices with their start and end apart: 18, of which 8 were waited for; matrix products, arithmetic and copies ran while one was open for 1% of the time, Pallas kernels for 6%

profile of v2, /device:TPU:99, one launch (start us, length us, event | category | flops | bytes accessed | tf_op | source)
XLA Modules:
  0.0 204.1 jit_solution(2592527370101889303)
XLA Ops:
  0.6 2.1 %collective-permute-start.6 = (bf16[512,256]{1,0:T(8,128)(2,1)}, bf16[512,256]{1,0:T(8,128)(2,1)S(1)}, u32[]{:S(2)}, u32[]{:S(2)}) collective-permute-start(bf16[512,256]{1,0:T(8,128)(2,1)} %bitcast.24), channel_id=1, source_target_pairs={{0,2},{1,3},{2,0},{3,1},{4,6},{5,7},{6,4},{7,5},{8,10},{9,11},{10,... | collective-permute-start | bytes 786440 | tf_op jit(solution)/shard_map/ppermute | solution.py:16
  2.7 1.1 dynamic-slice_bitcast_fusion
  3.8 1.9 collective-permute-start
  5.7 2.7 %collective-permute-start.5 = (bf16[512,256]{1,0:T(8,128)(2,1)}, bf16[512,256]{1,0:T(8,128)(2,1)S(1)}, u32[]{:S(2)}, u32[]{:S(2)}) collective-permute-start(bf16[512,256]{1,0:T(8,128)(2,1)} %bitcast.25), channel_id=1, source_target_pairs={{0,1},{1,0},{2,3},{3,2},{4,5},{5,4},{6,7},{7,6},{8,9},{9,8},{10,11... | collective-permute-start | bytes 786440 | tf_op jit(solution)/shard_map/ppermute | solution.py:16
  8.7 3.6 %collective-permute-start.2 = (bf16[512,1024]{1,0:T(8,128)(2,1)}, bf16[512,1024]{1,0:T(8,128)(2,1)}, u32[]{:S(2)}, u32[]{:S(2)}) collective-permute-start(bf16[512,1024]{1,0:T(8,128)(2,1)} %bitcast.3.w0), channel_id=1, source_target_pairs={{0,2},{1,3},{2,0},{3,1},{4,6},{5,7},{6,4},{7,5},{8,10},{9,11},{10,... | collective-permute-start | bytes 3145736 | tf_op jit(solution)/shard_map/ppermute | solution.py:16
  12.3 2.4 %collective-permute-start.7 = (bf16[512,256]{1,0:T(8,128)(2,1)S(1)}, bf16[512,256]{1,0:T(8,128)(2,1)S(1)}, u32[]{:S(2)}, u32[]{:S(2)}) collective-permute-start(bf16[512,256]{1,0:T(8,128)(2,1)S(1)} %collective-permute-done.6.w2), channel_id=1, source_target_pairs={{0,1},{1,0},{2,3},{3,2},{4,5},{5,4},{6,7},{7,6},{8,9},{9,8},{10,11... | collective-permute-start | bytes 786440 | tf_op jit(solution)/shard_map/ppermute | solution.py:16
  15.1 15.6 %collective-permute-done.far_ref.refs_2_ = bf16[128,2048]{1,0:T(8,128)(2,1)S(1)} collective-permute-done((bf16[128,2048]{1,0:T(8,128)(2,1)S(1)}, bf16[128,2048]{1,0:T(8,128)(2,1)S(1)}, u32[]{:S(2)}, u32[]{:S(2)}) %collective-permute-start) | collective-permute-done | bytes 524320 | tf_op jit(solution)/shard_map/ppermute | solution.py:16
  31.1 1.9 collective-permute-start.8
  33.2 10.0 %collective-permute-done.8.far_ref = bf16[128,256]{1,0:T(8,128)(2,1)S(1)} collective-permute-done((bf16[128,256]{1,0:T(8,128)(2,1)S(1)}, bf16[128,256]{1,0:T(8,128)(2,1)S(1)}, u32[]{:S(2)}, u32[]{:S(2)}) %collective-permute-start.8) | collective-permute-done | bytes 65568 | tf_op jit(solution)/shard_map/ppermute | solution.py:16
  44.1 7.1 %all-to-all-start = ((bf16[8,128,256]{2,1,0:T(8,128)(2,1)}), bf16[8,128,256]{2,1,0:T(8,128)(2,1)S(1)}, u32[]{:S(2)}, u32[]{:S(2)}) async-start(bf16[8,128,256]{2,1,0:T(8,128)(2,1)} %shard_map.89), calls=%async_computation | async-start | bytes 1048576 | tf_op jit(solution)/shard_map/all_to_all | solution.py:209
  51.2 2.3 %collective-permute-start.1 = (bf16[512,1024]{1,0:T(8,128)(2,1)}, bf16[512,1024]{1,0:T(8,128)(2,1)S(1)}, u32[]{:S(2)}, u32[]{:S(2)}) collective-permute-start(bf16[512,1024]{1,0:T(8,128)(2,1)} %bitcast.3.w0), channel_id=1, source_target_pairs={{0,1},{1,0},{2,3},{3,2},{4,5},{5,4},{6,7},{7,6},{8,9},{9,8},{10,11... | collective-permute-start | bytes 3145736 | tf_op jit(solution)/shard_map/ppermute | solution.py:16
  53.5 2.1 %collective-permute-start.3 = (bf16[512,1024]{1,0:T(8,128)(2,1)}, bf16[512,1024]{1,0:T(8,128)(2,1)S(1)}, u32[]{:S(2)}, u32[]{:S(2)}) collective-permute-start(bf16[512,1024]{1,0:T(8,128)(2,1)} %collective-permute-done.2.w2), channel_id=1, source_target_pairs={{0,1},{1,0},{2,3},{3,2},{4,5},{5,4},{6,7},{7,6},{8,9},{9,8},{10,11... | collective-permute-start | bytes 3145736 | tf_op jit(solution)/shard_map/ppermute | solution.py:16
  55.6 2.2 %collective-permute-start.10 = (bf16[1024,512]{1,0:T(8,128)(2,1)S(1)}, bf16[1024,512]{1,0:T(8,128)(2,1)}, u32[]{:S(2)}, u32[]{:S(2)}) collective-permute-start(bf16[1024,512]{1,0:T(8,128)(2,1)S(1)} %bitcast.19), channel_id=1, source_target_pairs={{0,2},{1,3},{2,0},{3,1},{4,6},{5,7},{6,4},{7,5},{8,10},{9,11},{10,... | collective-permute-start | bytes 3145736 | tf_op jit(solution)/shard_map/ppermute | solution.py:16
  58.3 2.8 %shard_map.87 = (f32[128,1024]{1,0:T(8,128)S(1)}, bf16[128,1024]{1,0:T(8,128)(2,1)S(1)}) custom-call(s32[1]{0:T(128)} %bitcast.place_ref.refs_0_, bf16[128,4096]{1,0:T(8,128)(2,1)S(1)} %bitcast.17, bf16[128,2048]{1,0:T(8,128)(2,1)S(1)} %collective-permute-done.far_ref.refs_2_, f32[1,4096]{1,0:T(1,128)S(1)} %copy-done.7, bf16[512,1024]{1,0:T(8,128)(2,1)} %bitcast.3.w0, ...), custom_call_target="tpu_custom_call" | custom-call | flops 1 | bytes 1 | tf_op jit(solution)/shard_map/pallas_call | solution.py:36
  61.9 2.3 %collective-permute-start.4 = (bf16[128,1024]{1,0:T(8,128)(2,1)S(1)}, bf16[128,1024]{1,0:T(8,128)(2,1)S(1)}, u32[]{:S(2)}, u32[]{:S(2)}) collective-permute-start(bf16[128,1024]{1,0:T(8,128)(2,1)S(1)} %get-tuple-element.19), channel_id=1, source_target_pairs={{0,4},{1,5},{2,6},{3,7},{4,0},{5,1},{6,2},{7,3},{8,12},{9,13},{10,... | collective-permute-start | bytes 786440 | tf_op jit(solution)/shard_map/ppermute | solution.py:16
  64.2 2.3 %collective-permute-start.9 = (bf16[1024,512]{1,0:T(8,128)(2,1)S(1)}, bf16[1024,512]{1,0:T(8,128)(2,1)}, u32[]{:S(2)}, u32[]{:S(2)}) collective-permute-start(bf16[1024,512]{1,0:T(8,128)(2,1)S(1)} %bitcast.20), channel_id=1, source_target_pairs={{0,1},{1,0},{2,3},{3,2},{4,5},{5,4},{6,7},{7,6},{8,9},{9,8},{10,11... | collective-permute-start | bytes 3145736 | tf_op jit(solution)/shard_map/ppermute | solution.py:16
  66.6 21.5 %collective-permute-done.4.far_ref = bf16[128,1024]{1,0:T(8,128)(2,1)S(1)} collective-permute-done((bf16[128,1024]{1,0:T(8,128)(2,1)S(1)}, bf16[128,1024]{1,0:T(8,128)(2,1)S(1)}, u32[]{:S(2)}, u32[]{:S(2)}) %collective-permute-start.4) | collective-permute-done | bytes 262176 | tf_op jit(solution)/shard_map/ppermute | solution.py:16
  88.8 1.0 copy-done.3
  90.8 3.0 %shard_map.90.refs_1_ = bf16[128,1024]{1,0:T(8,128)(2,1)S(1)} custom-call(s32[1]{0:T(128)} %bitcast.place_ref.refs_0_, f32[128,1024]{1,0:T(8,128)S(1)} %copy-done.3, bf16[128,1024]{1,0:T(8,128)(2,1)S(1)} %copy-done.6, f32[128,128]{1,0:T(8,128)S(1)} %shard_map.86.scale_ref, f32[128,128]{1,0:T(8,128)S(1)} %get-tuple-element.33.cos_ref, ...), custom_call_target="tpu_custom_call" | custom-call | flops 1 | bytes 1 | tf_op jit(solution)/shard_map/pallas_call | solution.py:36
  93.8 2.8 %collective-permute-start.11 = (bf16[1024,512]{1,0:T(8,128)(2,1)}, bf16[1024,512]{1,0:T(8,128)(2,1)S(1)}, u32[]{:S(2)}, u32[]{:S(2)}) collective-permute-start(bf16[1024,512]{1,0:T(8,128)(2,1)} %collective-permute-done.10.refs_5_), channel_id=1, source_target_pairs={{0,1},{1,0},{2,3},{3,2},{4,5},{5,4},{6,7},{7,6},{8,9},{9,8},{10,11... | collective-permute-start | bytes 3145736 | tf_op jit(solution)/shard_map/ppermute | solution.py:16
  96.6 5.0 %collective-permute-start.14 = (bf16[128,1024]{1,0:T(8,128)(2,1)S(1)}, bf16[128,1024]{1,0:T(8,128)(2,1)S(1)}, u32[]{:S(2)}, u32[]{:S(2)}) collective-permute-start(bf16[128,1024]{1,0:T(8,128)(2,1)S(1)} %shard_map.90.refs_1_), channel_id=1, source_target_pairs={{0,4},{1,5},{2,6},{3,7},{4,0},{5,1},{6,2},{7,3},{8,12},{9,13},{10,... | collective-permute-start | bytes 786440 | tf_op jit(solution)/shard_map/ppermute | solution.py:16
  101.6 2.3 %shard_map.91 = (bf16[64,2048]{1,0:T(8,128)(2,1)S(1)}, bf16[64,2048]{1,0:T(8,128)(2,1)S(1)}) custom-call(s32[1]{0:T(128)} %bitcast.place_ref.refs_0_, bf16[128,1024]{1,0:T(8,128)(2,1)S(1)} %shard_map.90.refs_1_, bf16[128,4096]{1,0:T(8,128)(2,1)S(1)} %bitcast.18, bf16[1024,512]{1,0:T(8,128)(2,1)S(1)} %bitcast.21, ...), custom_call_target="tpu_custom_call" | custom-call | flops 1 | bytes 1 | tf_op jit(solution)/shard_map/pallas_call | solution.py:36
  104.0 8.8 %collective-permute-start.12 = (bf16[64,2048]{1,0:T(8,128)(2,1)S(1)}, bf16[64,2048]{1,0:T(8,128)(2,1)S(1)}, u32[]{:S(2)}, u32[]{:S(2)}) collective-permute-start(bf16[64,2048]{1,0:T(8,128)(2,1)S(1)} %get-tuple-element.25), channel_id=1, source_target_pairs={{0,8},{1,9},{2,10},{3,11},{4,12},{5,13},{6,14},{7,15},{8,0},{9,1},... | collective-permute-start | bytes 786440 | tf_op jit(solution)/shard_map/ppermute | solution.py:24
  112.8 1.3 collective-permute-done.14.refs_1_
  114.1 2.3 %shard_map.92 = bf16[128,2048]{1,0:T(8,128)(2,1)S(1)} custom-call(s32[1]{0:T(128)} %bitcast.place_ref.refs_0_, bf16[128,1024]{1,0:T(8,128)(2,1)S(1)} %collective-permute-done.14.refs_1_, bf16[128,2048]{1,0:T(8,128)(2,1)S(1)} %collective-permute-done.far_ref.refs_2_, bf16[1024,512]{1,0:T(8,128)(2,1)S(1)} %bitcast.22, ...), custom_call_target="tpu_custom_call" | custom-call | flops 1 | bytes 1 | tf_op jit(solution)/shard_map/pallas_call | solution.py:36
  116.4 6.2 %collective-permute-start.15 = (bf16[128,2048]{1,0:T(8,128)(2,1)S(1)}, bf16[128,2048]{1,0:T(8,128)(2,1)S(1)}, u32[]{:S(2)}, u32[]{:S(2)}) collective-permute-start(bf16[128,2048]{1,0:T(8,128)(2,1)S(1)} %shard_map.92), channel_id=1, source_target_pairs={{0,12},{1,13},{2,14},{3,15},{4,8},{5,9},{6,10},{7,11},{8,4},{9,5},... | collective-permute-start | bytes 1572872 | tf_op jit(solution)/shard_map/ppermute | solution.py:24
  122.6 17.9 %collective-permute-start.16 = (bf16[512,128]{1,0:T(8,128)(2,1)S(1)}, bf16[512,128]{1,0:T(8,128)(2,1)S(1)}, u32[]{:S(2)}, u32[]{:S(2)}) collective-permute-start(bf16[512,128]{1,0:T(8,128)(2,1)S(1)} %bitcast.28), channel_id=1, source_target_pairs={{0,504},{8,496},{16,488},{24,480},{32,472},{40,464},{48,456},{56,4... | collective-permute-start | bytes 393224 | tf_op jit(solution)/shard_map/ppermute | solution.py:230
  140.6 45.6 %collective-permute-done.12.first = bf16[64,2048]{1,0:T(8,128)(2,1)S(1)} collective-permute-done((bf16[64,2048]{1,0:T(8,128)(2,1)S(1)}, bf16[64,2048]{1,0:T(8,128)(2,1)S(1)}, u32[]{:S(2)}, u32[]{:S(2)}) %collective-permute-start.12) | collective-permute-done | bytes 262176 | tf_op jit(solution)/shard_map/ppermute | solution.py:24
  186.2 8.0 %collective-permute-start.13 = (bf16[64,2048]{1,0:T(8,128)(2,1)S(1)}, bf16[64,2048]{1,0:T(8,128)(2,1)S(1)}, u32[]{:S(2)}, u32[]{:S(2)}) collective-permute-start(bf16[64,2048]{1,0:T(8,128)(2,1)S(1)} %get-tuple-element.27), channel_id=1, source_target_pairs={{0,8},{1,9},{2,10},{3,11},{4,12},{5,13},{6,14},{7,15},{8,0},{9,1},... | collective-permute-start | bytes 786440 | tf_op jit(solution)/shard_map/ppermute | solution.py:24
  194.9 2.5 %collective-permute-done.15.far = bf16[128,2048]{1,0:T(8,128)(2,1)S(1)} collective-permute-done((bf16[128,2048]{1,0:T(8,128)(2,1)S(1)}, bf16[128,2048]{1,0:T(8,128)(2,1)S(1)}, u32[]{:S(2)}, u32[]{:S(2)}) %collective-permute-start.15) | collective-permute-done | bytes 524320 | tf_op jit(solution)/shard_map/ppermute | solution.py:24
  197.4 5.6 %collective-permute-done.13.second = bf16[64,2048]{1,0:T(8,128)(2,1)S(1)} collective-permute-done((bf16[64,2048]{1,0:T(8,128)(2,1)S(1)}, bf16[64,2048]{1,0:T(8,128)(2,1)S(1)}, u32[]{:S(2)}, u32[]{:S(2)}) %collective-permute-start.13) | collective-permute-done | bytes 262176 | tf_op jit(solution)/shard_map/ppermute | solution.py:24
  203.0 1.0 shard_map.93
  (38 shorter events, 5.7 us)
Async XLA Ops:
  0.6 7.8 %copy-start = (bf16[1,128,4096]{2,1,0:T(8,128)(2,1)S(1)}, bf16[1,128,4096]{2,1,0:T(8,128)(2,1)}, u32[]{:S(2)}) copy-start(bf16[1,128,4096]{2,1,0:T(8,128)(2,1)} %param.7) | copy-start | bytes 3145732
  0.6 11.7 %collective-permute-start.6 = (bf16[512,256]{1,0:T(8,128)(2,1)}, bf16[512,256]{1,0:T(8,128)(2,1)S(1)}, u32[]{:S(2)}, u32[]{:S(2)}) collective-permute-start(bf16[512,256]{1,0:T(8,128)(2,1)} %bitcast.24), channel_id=1, source_target_pairs={{0,2},{1,3},{2,0},{3,1},{4,6},{5,7},{6,4},{7,5},{8,10},{9,11},{10,... | collective-permute-start | bytes 786440 | tf_op jit(solution)/shard_map/ppermute | solution.py:16
  3.8 26.9 %collective-permute-start = (bf16[128,2048]{1,0:T(8,128)(2,1)S(1)}, bf16[128,2048]{1,0:T(8,128)(2,1)S(1)}, u32[]{:S(2)}, u32[]{:S(2)}) collective-permute-start(bf16[128,2048]{1,0:T(8,128)(2,1)S(1)} %dynamic-slice_bitcast_fusion), channel_id=1, source_target_pairs={{0,4},{1,5},{2,6},{3,7},{4,0},{5,1},{6,2},{7,3},{8,12},{9,13},{10,... | collective-permute-start | bytes 1572872 | tf_op jit(solution)/shard_map/ppermute | solution.py:16
  5.7 9.3 %collective-permute-start.5 = (bf16[512,256]{1,0:T(8,128)(2,1)}, bf16[512,256]{1,0:T(8,128)(2,1)S(1)}, u32[]{:S(2)}, u32[]{:S(2)}) collective-permute-start(bf16[512,256]{1,0:T(8,128)(2,1)} %bitcast.25), channel_id=1, source_target_pairs={{0,1},{1,0},{2,3},{3,2},{4,5},{5,4},{6,7},{7,6},{8,9},{9,8},{10,11... | collective-permute-start | bytes 786440 | tf_op jit(solution)/shard_map/ppermute | solution.py:16
  8.4 22.2 %copy-start.4 = (bf16[1,512,256]{2,1,0:T(8,128)(2,1)S(1)}, bf16[1,512,256]{2,1,0:T(8,128)(2,1)}, u32[]{:S(2)}) copy-start(bf16[1,512,256]{2,1,0:T(8,128)(2,1)} %param.10) | copy-start | bytes 786436
  8.7 44.8 %collective-permute-start.2 = (bf16[512,1024]{1,0:T(8,128)(2,1)}, bf16[512,1024]{1,0:T(8,128)(2,1)}, u32[]{:S(2)}, u32[]{:S(2)}) collective-permute-start(bf16[512,1024]{1,0:T(8,128)(2,1)} %bitcast.3.w0), channel_id=1, source_target_pairs={{0,2},{1,3},{2,0},{3,1},{4,6},{5,7},{6,4},{7,5},{8,10},{9,11},{10,... | collective-permute-start | bytes 3145736 | tf_op jit(solution)/shard_map/ppermute | solution.py:16
  12.3 18.4 %collective-permute-start.7 = (bf16[512,256]{1,0:T(8,128)(2,1)S(1)}, bf16[512,256]{1,0:T(8,128)(2,1)S(1)}, u32[]{:S(2)}, u32[]{:S(2)}) collective-permute-start(bf16[512,256]{1,0:T(8,128)(2,1)S(1)} %collective-permute-done.6.w2), channel_id=1, source_target_pairs={{0,1},{1,0},{2,3},{3,2},{4,5},{5,4},{6,7},{7,6},{8,9},{9,8},{10,11... | collective-permute-start | bytes 786440 | tf_op jit(solution)/shard_map/ppermute | solution.py:16
  14.7 15.9 %copy-start.7 = (f32[1,4096]{1,0:T(1,128)S(1)}, f32[1,4096]{1,0:T(1,128)}, u32[]{:S(2)}) copy-start(f32[1,4096]{1,0:T(1,128)} %gain_ref.3) | copy-start | bytes 49156
  31.1 12.1 %collective-permute-start.8 = (bf16[128,256]{1,0:T(8,128)(2,1)S(1)}, bf16[128,256]{1,0:T(8,128)(2,1)S(1)}, u32[]{:S(2)}, u32[]{:S(2)}) collective-permute-start(bf16[128,256]{1,0:T(8,128)(2,1)S(1)} %get-tuple-element.21), channel_id=1, source_target_pairs={{0,4},{1,5},{2,6},{3,7},{4,0},{5,1},{6,2},{7,3},{8,12},{9,13},{10,... | collective-permute-start | bytes 196616 | tf_op jit(solution)/shard_map/ppermute | solution.py:16
  33.2 22.4 %copy-start.1 = (bf16[1,1024,512]{2,1,0:T(8,128)(2,1)S(1)}, bf16[1,1024,512]{2,1,0:T(8,128)(2,1)}, u32[]{:S(2)}) copy-start(bf16[1,1024,512]{2,1,0:T(8,128)(2,1)} %param.11) | copy-start | bytes 3145732
  44.1 44.6 %all-to-all-start = ((bf16[8,128,256]{2,1,0:T(8,128)(2,1)}), bf16[8,128,256]{2,1,0:T(8,128)(2,1)S(1)}, u32[]{:S(2)}, u32[]{:S(2)}) async-start(bf16[8,128,256]{2,1,0:T(8,128)(2,1)} %shard_map.89), calls=%async_computation | async-start | bytes 1048576 | tf_op jit(solution)/shard_map/all_to_all | solution.py:209
  51.2 6.6 %collective-permute-start.1 = (bf16[512,1024]{1,0:T(8,128)(2,1)}, bf16[512,1024]{1,0:T(8,128)(2,1)S(1)}, u32[]{:S(2)}, u32[]{:S(2)}) collective-permute-start(bf16[512,1024]{1,0:T(8,128)(2,1)} %bitcast.3.w0), channel_id=1, source_target_pairs={{0,1},{1,0},{2,3},{3,2},{4,5},{5,4},{6,7},{7,6},{8,9},{9,8},{10,11... | collective-permute-start | bytes 3145736 | tf_op jit(solution)/shard_map/ppermute | solution.py:16
  53.5 4.8 %collective-permute-start.3 = (bf16[512,1024]{1,0:T(8,128)(2,1)}, bf16[512,1024]{1,0:T(8,128)(2,1)S(1)}, u32[]{:S(2)}, u32[]{:S(2)}) collective-permute-start(bf16[512,1024]{1,0:T(8,128)(2,1)} %collective-permute-done.2.w2), channel_id=1, source_target_pairs={{0,1},{1,0},{2,3},{3,2},{4,5},{5,4},{6,7},{7,6},{8,9},{9,8},{10,11... | collective-permute-start | bytes 3145736 | tf_op jit(solution)/shard_map/ppermute | solution.py:16
  55.6 38.2 %collective-permute-start.10 = (bf16[1024,512]{1,0:T(8,128)(2,1)S(1)}, bf16[1024,512]{1,0:T(8,128)(2,1)}, u32[]{:S(2)}, u32[]{:S(2)}) collective-permute-start(bf16[1024,512]{1,0:T(8,128)(2,1)S(1)} %bitcast.19), channel_id=1, source_target_pairs={{0,2},{1,3},{2,0},{3,1},{4,6},{5,7},{6,4},{7,5},{8,10},{9,11},{10,... | collective-permute-start | bytes 3145736 | tf_op jit(solution)/shard_map/ppermute | solution.py:16
  61.1 0.8 copy-start.2
  61.9 26.2 %collective-permute-start.4 = (bf16[128,1024]{1,0:T(8,128)(2,1)S(1)}, bf16[128,1024]{1,0:T(8,128)(2,1)S(1)}, u32[]{:S(2)}, u32[]{:S(2)}) collective-permute-start(bf16[128,1024]{1,0:T(8,128)(2,1)S(1)} %get-tuple-element.19), channel_id=1, source_target_pairs={{0,4},{1,5},{2,6},{3,7},{4,0},{5,1},{6,2},{7,3},{8,12},{9,13},{10,... | collective-permute-start | bytes 786440 | tf_op jit(solution)/shard_map/ppermute | solution.py:16
  64.2 37.4 %collective-permute-start.9 = (bf16[1024,512]{1,0:T(8,128)(2,1)S(1)}, bf16[1024,512]{1,0:T(8,128)(2,1)}, u32[]{:S(2)}, u32[]{:S(2)}) collective-permute-start(bf16[1024,512]{1,0:T(8,128)(2,1)S(1)} %bitcast.20), channel_id=1, source_target_pairs={{0,1},{1,0},{2,3},{3,2},{4,5},{5,4},{6,7},{7,6},{8,9},{9,8},{10,11... | collective-permute-start | bytes 3145736 | tf_op jit(solution)/shard_map/ppermute | solution.py:16
  88.1 0.7 copy-start.5
  88.8 1.0 copy-start.3
  89.8 0.9 copy-start.6
  93.8 7.8 %collective-permute-start.11 = (bf16[1024,512]{1,0:T(8,128)(2,1)}, bf16[1024,512]{1,0:T(8,128)(2,1)S(1)}, u32[]{:S(2)}, u32[]{:S(2)}) collective-permute-start(bf16[1024,512]{1,0:T(8,128)(2,1)} %collective-permute-done.10.refs_5_), channel_id=1, source_target_pairs={{0,1},{1,0},{2,3},{3,2},{4,5},{5,4},{6,7},{7,6},{8,9},{9,8},{10,11... | collective-permute-start | bytes 3145736 | tf_op jit(solution)/shard_map/ppermute | solution.py:16
  96.6 17.5 %collective-permute-start.14 = (bf16[128,1024]{1,0:T(8,128)(2,1)S(1)}, bf16[128,1024]{1,0:T(8,128)(2,1)S(1)}, u32[]{:S(2)}, u32[]{:S(2)}) collective-permute-start(bf16[128,1024]{1,0:T(8,128)(2,1)S(1)} %shard_map.90.refs_1_), channel_id=1, source_target_pairs={{0,4},{1,5},{2,6},{3,7},{4,0},{5,1},{6,2},{7,3},{8,12},{9,13},{10,... | collective-permute-start | bytes 786440 | tf_op jit(solution)/shard_map/ppermute | solution.py:16
  104.0 82.2 %collective-permute-start.12 = (bf16[64,2048]{1,0:T(8,128)(2,1)S(1)}, bf16[64,2048]{1,0:T(8,128)(2,1)S(1)}, u32[]{:S(2)}, u32[]{:S(2)}) collective-permute-start(bf16[64,2048]{1,0:T(8,128)(2,1)S(1)} %get-tuple-element.25), channel_id=1, source_target_pairs={{0,8},{1,9},{2,10},{3,11},{4,12},{5,13},{6,14},{7,15},{8,0},{9,1},... | collective-permute-start | bytes 786440 | tf_op jit(solution)/shard_map/ppermute | solution.py:24
  114.1 8.5 %copy-start.9 = (bf16[1,512,128]{2,1,0:T(8,128)(2,1)S(1)}, bf16[1,512,128]{2,1,0:T(8,128)(2,1)}, u32[]{:S(2)}) copy-start(bf16[1,512,128]{2,1,0:T(8,128)(2,1)} %param.13) | copy-start | bytes 393220
  114.1 80.1 %copy-start.8 = (bf16[1,512,128]{2,1,0:T(8,128)(2,1)S(1)}, bf16[1,512,128]{2,1,0:T(8,128)(2,1)}, u32[]{:S(2)}) copy-start(bf16[1,512,128]{2,1,0:T(8,128)(2,1)} %param.12) | copy-start | bytes 393220
  116.4 81.0 %collective-permute-start.15 = (bf16[128,2048]{1,0:T(8,128)(2,1)S(1)}, bf16[128,2048]{1,0:T(8,128)(2,1)S(1)}, u32[]{:S(2)}, u32[]{:S(2)}) collective-permute-start(bf16[128,2048]{1,0:T(8,128)(2,1)S(1)} %shard_map.92), channel_id=1, source_target_pairs={{0,12},{1,13},{2,14},{3,15},{4,8},{5,9},{6,10},{7,11},{8,4},{9,5},... | collective-permute-start | bytes 1572872 | tf_op jit(solution)/shard_map/ppermute | solution.py:24
  122.6 71.6 %collective-permute-start.16 = (bf16[512,128]{1,0:T(8,128)(2,1)S(1)}, bf16[512,128]{1,0:T(8,128)(2,1)S(1)}, u32[]{:S(2)}, u32[]{:S(2)}) collective-permute-start(bf16[512,128]{1,0:T(8,128)(2,1)S(1)} %bitcast.28), channel_id=1, source_target_pairs={{0,504},{8,496},{16,488},{24,480},{32,472},{40,464},{48,456},{56,4... | collective-permute-start | bytes 393224 | tf_op jit(solution)/shard_map/ppermute | solution.py:230
  186.2 16.9 %collective-permute-start.13 = (bf16[64,2048]{1,0:T(8,128)(2,1)S(1)}, bf16[64,2048]{1,0:T(8,128)(2,1)S(1)}, u32[]{:S(2)}, u32[]{:S(2)}) collective-permute-start(bf16[64,2048]{1,0:T(8,128)(2,1)S(1)} %get-tuple-element.27), channel_id=1, source_target_pairs={{0,8},{1,9},{2,10},{3,11},{4,12},{5,13},{6,14},{7,15},{8,0},{9,1},... | collective-permute-start | bytes 786440 | tf_op jit(solution)/shard_map/ppermute | solution.py:24

commit v3 on v2

--- a/solution.py
+++ b/solution.py
@@ -77,7 +77,7 @@
     near, far = project(
         place_ref[0], own_ref, far_ref, gain_ref, (w0, w1, w2, w3), (0, 1, 2, 3)
     )
-    near_out[...] = near
+    near_out[...] = near.astype(near_out.dtype)
     far_out[...] = far.astype(jnp.bfloat16)
 
 
@@ -112,7 +112,7 @@
     sine = sin_ref[...]
     for head in range(width // size):
         cols = slice(head * size, (head + 1) * size)
-        total = (near_ref[:, cols] + far_ref[:, cols].astype(jnp.float32)) * scale
+        total = (near_ref[:, cols].astype(jnp.float32) + far_ref[:, cols].astype(jnp.float32)) * scale
         query = rope(total, cosine, sine).astype(jnp.bfloat16)
         scores = lax.dot_general(
             query, keys, (((1,), (1,)), ((), ())), preferred_element_type=jnp.float32
@@ -198,7 +198,7 @@
     far = exchange(far, 4)
     query_near, query_far = call(
         project_kernel,
-        (array(tokens, wide, f32), array(tokens, wide)),
+        (array(tokens, wide), array(tokens, wide)),
         place, rows, far_rows, norm_gain, w_query, query_1, query_2, query_3,
     )
     keyval = call(

time: 205 us -> 205 us (level)
    unnamed x20 -> x22, local copies, waits for them, and re-layouts: 3.51 us -> 4.14 us
where the time goes in v3:
time: 205 us; the launch traced here: 204 us
  waiting for transfers between devices  103 us (50%)
  starting transfers between devices  81.6 us (40%)
  Pallas kernels  12.4 us (6%)
  local copies, waits for them, and re-layouts  5.22 us (3%)
    ppermute x3, waiting for transfers between devices, across(): return lax.ppermute(x, ('section', 'seq'), pairs)  53.7 us
    ppermute x13, waiting for transfers between devices, exchange(): return lax.ppermute(x, 'seq', [(i, i ^ flip) for i in range(size)])  49 us
    ppermute x13, starting transfers between devices, exchange(): return lax.ppermute(x, 'seq', [(i, i ^ flip) for i in range(size)])  33.5 us
    ppermute x3, starting transfers between devices, across(): return lax.ppermute(x, ('section', 'seq'), pairs)  22.9 us
    ppermute x1, starting transfers between devices, shards(): lax.ppermute(after(up_grads[0], far), 'section', [(i, sections - 1 - i) f...  18.1 us
    pallas_call x8, Pallas kernels, call(): pl.pallas_call(kernel, out_shape=outs, in_specs=[pl.BlockSpec(memory_spac...  12.4 us
    all_to_all x1, starting transfers between devices, shards(): lax.all_to_all(keyval, 'seq', split_axis=0, concat_axis=0, tiled=True)  7.09 us
    unnamed x22, local copies, waits for them, and re-layouts  4.14 us
  transfers between devices with their start and end apart: 18, of which 8 were waited for; matrix products, arithmetic and copies ran while one was open for 1% of the time, Pallas kernels for 6%

profile of v3, /device:TPU:99, one launch (start us, length us, event | category | flops | bytes accessed | tf_op | source)
XLA Modules:
  0.0 204.0 jit_solution(14386934293042338122)
XLA Ops:
  0.6 2.1 %collective-permute-start.6 = (bf16[512,256]{1,0:T(8,128)(2,1)}, bf16[512,256]{1,0:T(8,128)(2,1)S(1)}, u32[]{:S(2)}, u32[]{:S(2)}) collective-permute-start(bf16[512,256]{1,0:T(8,128)(2,1)} %bitcast.24), channel_id=1, source_target_pairs={{0,2},{1,3},{2,0},{3,1},{4,6},{5,7},{6,4},{7,5},{8,10},{9,11},{10,... | collective-permute-start | bytes 786440 | tf_op jit(solution)/shard_map/ppermute | solution.py:16
  2.7 1.1 dynamic-slice_bitcast_fusion
  3.8 1.9 collective-permute-start
  5.7 2.7 %collective-permute-start.5 = (bf16[512,256]{1,0:T(8,128)(2,1)}, bf16[512,256]{1,0:T(8,128)(2,1)S(1)}, u32[]{:S(2)}, u32[]{:S(2)}) collective-permute-start(bf16[512,256]{1,0:T(8,128)(2,1)} %bitcast.25), channel_id=1, source_target_pairs={{0,1},{1,0},{2,3},{3,2},{4,5},{5,4},{6,7},{7,6},{8,9},{9,8},{10,11... | collective-permute-start | bytes 786440 | tf_op jit(solution)/shard_map/ppermute | solution.py:16
  8.7 3.6 %collective-permute-start.2 = (bf16[512,1024]{1,0:T(8,128)(2,1)}, bf16[512,1024]{1,0:T(8,128)(2,1)}, u32[]{:S(2)}, u32[]{:S(2)}) collective-permute-start(bf16[512,1024]{1,0:T(8,128)(2,1)} %bitcast.3.w0), channel_id=1, source_target_pairs={{0,2},{1,3},{2,0},{3,1},{4,6},{5,7},{6,4},{7,5},{8,10},{9,11},{10,... | collective-permute-start | bytes 3145736 | tf_op jit(solution)/shard_map/ppermute | solution.py:16
  12.3 2.4 %collective-permute-start.7 = (bf16[512,256]{1,0:T(8,128)(2,1)S(1)}, bf16[512,256]{1,0:T(8,128)(2,1)S(1)}, u32[]{:S(2)}, u32[]{:S(2)}) collective-permute-start(bf16[512,256]{1,0:T(8,128)(2,1)S(1)} %collective-permute-done.6.w2), channel_id=1, source_target_pairs={{0,1},{1,0},{2,3},{3,2},{4,5},{5,4},{6,7},{7,6},{8,9},{9,8},{10,11... | collective-permute-start | bytes 786440 | tf_op jit(solution)/shard_map/ppermute | solution.py:16
  15.1 15.6 %collective-permute-done.far_ref.refs_2_ = bf16[128,2048]{1,0:T(8,128)(2,1)S(1)} collective-permute-done((bf16[128,2048]{1,0:T(8,128)(2,1)S(1)}, bf16[128,2048]{1,0:T(8,128)(2,1)S(1)}, u32[]{:S(2)}, u32[]{:S(2)}) %collective-permute-start) | collective-permute-done | bytes 524320 | tf_op jit(solution)/shard_map/ppermute | solution.py:16
  31.1 1.9 collective-permute-start.8
  33.2 10.0 %collective-permute-done.8.far_ref = bf16[128,256]{1,0:T(8,128)(2,1)S(1)} collective-permute-done((bf16[128,256]{1,0:T(8,128)(2,1)S(1)}, bf16[128,256]{1,0:T(8,128)(2,1)S(1)}, u32[]{:S(2)}, u32[]{:S(2)}) %collective-permute-start.8) | collective-permute-done | bytes 65568 | tf_op jit(solution)/shard_map/ppermute | solution.py:16
  44.1 7.1 %all-to-all-start = ((bf16[8,128,256]{2,1,0:T(8,128)(2,1)}), bf16[8,128,256]{2,1,0:T(8,128)(2,1)S(1)}, u32[]{:S(2)}, u32[]{:S(2)}) async-start(bf16[8,128,256]{2,1,0:T(8,128)(2,1)} %copy-done.2), calls=%async_computation | async-start | bytes 1048576 | tf_op jit(solution)/shard_map/all_to_all | solution.py:209
  51.2 2.3 %collective-permute-start.1 = (bf16[512,1024]{1,0:T(8,128)(2,1)}, bf16[512,1024]{1,0:T(8,128)(2,1)S(1)}, u32[]{:S(2)}, u32[]{:S(2)}) collective-permute-start(bf16[512,1024]{1,0:T(8,128)(2,1)} %bitcast.3.w0), channel_id=1, source_target_pairs={{0,1},{1,0},{2,3},{3,2},{4,5},{5,4},{6,7},{7,6},{8,9},{9,8},{10,11... | collective-permute-start | bytes 3145736 | tf_op jit(solution)/shard_map/ppermute | solution.py:16
  53.5 2.1 %collective-permute-start.3 = (bf16[512,1024]{1,0:T(8,128)(2,1)}, bf16[512,1024]{1,0:T(8,128)(2,1)S(1)}, u32[]{:S(2)}, u32[]{:S(2)}) collective-permute-start(bf16[512,1024]{1,0:T(8,128)(2,1)} %collective-permute-done.2.w2), channel_id=1, source_target_pairs={{0,1},{1,0},{2,3},{3,2},{4,5},{5,4},{6,7},{7,6},{8,9},{9,8},{10,11... | collective-permute-start | bytes 3145736 | tf_op jit(solution)/shard_map/ppermute | solution.py:16
  55.6 2.2 %collective-permute-start.10 = (bf16[1024,512]{1,0:T(8,128)(2,1)S(1)}, bf16[1024,512]{1,0:T(8,128)(2,1)}, u32[]{:S(2)}, u32[]{:S(2)}) collective-permute-start(bf16[1024,512]{1,0:T(8,128)(2,1)S(1)} %bitcast.19), channel_id=1, source_target_pairs={{0,2},{1,3},{2,0},{3,1},{4,6},{5,7},{6,4},{7,5},{8,10},{9,11},{10,... | collective-permute-start | bytes 3145736 | tf_op jit(solution)/shard_map/ppermute | solution.py:16
  58.3 2.8 %shard_map.87 = (bf16[128,1024]{1,0:T(8,128)(2,1)S(1)}, bf16[128,1024]{1,0:T(8,128)(2,1)S(1)}) custom-call(s32[1]{0:T(128)} %bitcast.place_ref.refs_0_, bf16[128,4096]{1,0:T(8,128)(2,1)S(1)} %bitcast.17, bf16[128,2048]{1,0:T(8,128)(2,1)S(1)} %collective-permute-done.far_ref.refs_2_, f32[1,4096]{1,0:T(1,128)S(1)} %copy-done.8, bf16[512,1024]{1,0:T(8,128)(2,1)} %bitcast.3.w0, ...), custom_call_target="tpu_custom_call" | custom-call | flops 1 | bytes 1 | tf_op jit(solution)/shard_map/pallas_call | solution.py:36
  61.8 2.3 %collective-permute-start.4 = (bf16[128,1024]{1,0:T(8,128)(2,1)S(1)}, bf16[128,1024]{1,0:T(8,128)(2,1)S(1)}, u32[]{:S(2)}, u32[]{:S(2)}) collective-permute-start(bf16[128,1024]{1,0:T(8,128)(2,1)S(1)} %get-tuple-element.19), channel_id=1, source_target_pairs={{0,4},{1,5},{2,6},{3,7},{4,0},{5,1},{6,2},{7,3},{8,12},{9,13},{10,... | collective-permute-start | bytes 786440 | tf_op jit(solution)/shard_map/ppermute | solution.py:16
  64.1 2.3 %collective-permute-start.9 = (bf16[1024,512]{1,0:T(8,128)(2,1)S(1)}, bf16[1024,512]{1,0:T(8,128)(2,1)}, u32[]{:S(2)}, u32[]{:S(2)}) collective-permute-start(bf16[1024,512]{1,0:T(8,128)(2,1)S(1)} %bitcast.20), channel_id=1, source_target_pairs={{0,1},{1,0},{2,3},{3,2},{4,5},{5,4},{6,7},{7,6},{8,9},{9,8},{10,11... | collective-permute-start | bytes 3145736 | tf_op jit(solution)/shard_map/ppermute | solution.py:16
  66.5 21.6 %collective-permute-done.4.far_ref = bf16[128,1024]{1,0:T(8,128)(2,1)S(1)} collective-permute-done((bf16[128,1024]{1,0:T(8,128)(2,1)S(1)}, bf16[128,1024]{1,0:T(8,128)(2,1)S(1)}, u32[]{:S(2)}, u32[]{:S(2)}) %collective-permute-start.4) | collective-permute-done | bytes 262176 | tf_op jit(solution)/shard_map/ppermute | solution.py:16
  88.8 0.9 copy-done.5
  90.7 3.0 %shard_map.90.refs_1_ = bf16[128,1024]{1,0:T(8,128)(2,1)S(1)} custom-call(s32[1]{0:T(128)} %bitcast.place_ref.refs_0_, bf16[128,1024]{1,0:T(8,128)(2,1)S(1)} %copy-done.5, bf16[128,1024]{1,0:T(8,128)(2,1)S(1)} %copy-done.7, f32[128,128]{1,0:T(8,128)S(1)} %shard_map.86.scale_ref, f32[128,128]{1,0:T(8,128)S(1)} %get-tuple-element.33.cos_ref, ...), custom_call_target="tpu_custom_call" | custom-call | flops 1 | bytes 1 | tf_op jit(solution)/shard_map/pallas_call | solution.py:36
  93.7 2.8 %collective-permute-start.11 = (bf16[1024,512]{1,0:T(8,128)(2,1)}, bf16[1024,512]{1,0:T(8,128)(2,1)S(1)}, u32[]{:S(2)}, u32[]{:S(2)}) collective-permute-start(bf16[1024,512]{1,0:T(8,128)(2,1)} %collective-permute-done.10.refs_5_), channel_id=1, source_target_pairs={{0,1},{1,0},{2,3},{3,2},{4,5},{5,4},{6,7},{7,6},{8,9},{9,8},{10,11... | collective-permute-start | bytes 3145736 | tf_op jit(solution)/shard_map/ppermute | solution.py:16
  96.5 5.0 %collective-permute-start.14 = (bf16[128,1024]{1,0:T(8,128)(2,1)S(1)}, bf16[128,1024]{1,0:T(8,128)(2,1)S(1)}, u32[]{:S(2)}, u32[]{:S(2)}) collective-permute-start(bf16[128,1024]{1,0:T(8,128)(2,1)S(1)} %shard_map.90.refs_1_), channel_id=1, source_target_pairs={{0,4},{1,5},{2,6},{3,7},{4,0},{5,1},{6,2},{7,3},{8,12},{9,13},{10,... | collective-permute-start | bytes 786440 | tf_op jit(solution)/shard_map/ppermute | solution.py:16
  101.5 2.3 %shard_map.91 = (bf16[64,2048]{1,0:T(8,128)(2,1)S(1)}, bf16[64,2048]{1,0:T(8,128)(2,1)S(1)}) custom-call(s32[1]{0:T(128)} %bitcast.place_ref.refs_0_, bf16[128,1024]{1,0:T(8,128)(2,1)S(1)} %shard_map.90.refs_1_, bf16[128,4096]{1,0:T(8,128)(2,1)S(1)} %bitcast.18, bf16[1024,512]{1,0:T(8,128)(2,1)S(1)} %bitcast.21, ...), custom_call_target="tpu_custom_call" | custom-call | flops 1 | bytes 1 | tf_op jit(solution)/shard_map/pallas_call | solution.py:36
  103.9 8.8 %collective-permute-start.12 = (bf16[64,2048]{1,0:T(8,128)(2,1)S(1)}, bf16[64,2048]{1,0:T(8,128)(2,1)S(1)}, u32[]{:S(2)}, u32[]{:S(2)}) collective-permute-start(bf16[64,2048]{1,0:T(8,128)(2,1)S(1)} %get-tuple-element.25), channel_id=1, source_target_pairs={{0,8},{1,9},{2,10},{3,11},{4,12},{5,13},{6,14},{7,15},{8,0},{9,1},... | collective-permute-start | bytes 786440 | tf_op jit(solution)/shard_map/ppermute | solution.py:24
  112.7 1.3 collective-permute-done.14.refs_1_
  114.0 2.4 %shard_map.92 = bf16[128,2048]{1,0:T(8,128)(2,1)S(1)} custom-call(s32[1]{0:T(128)} %bitcast.place_ref.refs_0_, bf16[128,1024]{1,0:T(8,128)(2,1)S(1)} %collective-permute-done.14.refs_1_, bf16[128,2048]{1,0:T(8,128)(2,1)S(1)} %collective-permute-done.far_ref.refs_2_, bf16[1024,512]{1,0:T(8,128)(2,1)S(1)} %bitcast.22, ...), custom_call_target="tpu_custom_call" | custom-call | flops 1 | bytes 1 | tf_op jit(solution)/shard_map/pallas_call | solution.py:36
  116.4 6.0 %collective-permute-start.15 = (bf16[128,2048]{1,0:T(8,128)(2,1)S(1)}, bf16[128,2048]{1,0:T(8,128)(2,1)S(1)}, u32[]{:S(2)}, u32[]{:S(2)}) collective-permute-start(bf16[128,2048]{1,0:T(8,128)(2,1)S(1)} %shard_map.92), channel_id=1, source_target_pairs={{0,12},{1,13},{2,14},{3,15},{4,8},{5,9},{6,10},{7,11},{8,4},{9,5},... | collective-permute-start | bytes 1572872 | tf_op jit(solution)/shard_map/ppermute | solution.py:24
  122.4 18.1 %collective-permute-start.16 = (bf16[512,128]{1,0:T(8,128)(2,1)S(1)}, bf16[512,128]{1,0:T(8,128)(2,1)S(1)}, u32[]{:S(2)}, u32[]{:S(2)}) collective-permute-start(bf16[512,128]{1,0:T(8,128)(2,1)S(1)} %bitcast.28), channel_id=1, source_target_pairs={{0,504},{8,496},{16,488},{24,480},{32,472},{40,464},{48,456},{56,4... | collective-permute-start | bytes 393224 | tf_op jit(solution)/shard_map/ppermute | solution.py:230
  140.5 45.6 %collective-permute-done.12.first = bf16[64,2048]{1,0:T(8,128)(2,1)S(1)} collective-permute-done((bf16[64,2048]{1,0:T(8,128)(2,1)S(1)}, bf16[64,2048]{1,0:T(8,128)(2,1)S(1)}, u32[]{:S(2)}, u32[]{:S(2)}) %collective-permute-start.12) | collective-permute-done | bytes 262176 | tf_op jit(solution)/shard_map/ppermute | solution.py:24
  186.1 8.0 %collective-permute-start.13 = (bf16[64,2048]{1,0:T(8,128)(2,1)S(1)}, bf16[64,2048]{1,0:T(8,128)(2,1)S(1)}, u32[]{:S(2)}, u32[]{:S(2)}) collective-permute-start(bf16[64,2048]{1,0:T(8,128)(2,1)S(1)} %get-tuple-element.27), channel_id=1, source_target_pairs={{0,8},{1,9},{2,10},{3,11},{4,12},{5,13},{6,14},{7,15},{8,0},{9,1},... | collective-permute-start | bytes 786440 | tf_op jit(solution)/shard_map/ppermute | solution.py:24
  194.8 2.5 %collective-permute-done.15.far = bf16[128,2048]{1,0:T(8,128)(2,1)S(1)} collective-permute-done((bf16[128,2048]{1,0:T(8,128)(2,1)S(1)}, bf16[128,2048]{1,0:T(8,128)(2,1)S(1)}, u32[]{:S(2)}, u32[]{:S(2)}) %collective-permute-start.15) | collective-permute-done | bytes 524320 | tf_op jit(solution)/shard_map/ppermute | solution.py:24
  197.3 5.6 %collective-permute-done.13.second = bf16[64,2048]{1,0:T(8,128)(2,1)S(1)} collective-permute-done((bf16[64,2048]{1,0:T(8,128)(2,1)S(1)}, bf16[64,2048]{1,0:T(8,128)(2,1)S(1)}, u32[]{:S(2)}, u32[]{:S(2)}) %collective-permute-start.13) | collective-permute-done | bytes 262176 | tf_op jit(solution)/shard_map/ppermute | solution.py:24
  203.0 1.0 shard_map.93
  (40 shorter events, 5.7 us)
Async XLA Ops:
  0.6 7.8 %copy-start = (bf16[1,128,4096]{2,1,0:T(8,128)(2,1)S(1)}, bf16[1,128,4096]{2,1,0:T(8,128)(2,1)}, u32[]{:S(2)}) copy-start(bf16[1,128,4096]{2,1,0:T(8,128)(2,1)} %param.7) | copy-start | bytes 3145732
  0.6 11.7 %collective-permute-start.6 = (bf16[512,256]{1,0:T(8,128)(2,1)}, bf16[512,256]{1,0:T(8,128)(2,1)S(1)}, u32[]{:S(2)}, u32[]{:S(2)}) collective-permute-start(bf16[512,256]{1,0:T(8,128)(2,1)} %bitcast.24), channel_id=1, source_target_pairs={{0,2},{1,3},{2,0},{3,1},{4,6},{5,7},{6,4},{7,5},{8,10},{9,11},{10,... | collective-permute-start | bytes 786440 | tf_op jit(solution)/shard_map/ppermute | solution.py:16
  3.8 26.9 %collective-permute-start = (bf16[128,2048]{1,0:T(8,128)(2,1)S(1)}, bf16[128,2048]{1,0:T(8,128)(2,1)S(1)}, u32[]{:S(2)}, u32[]{:S(2)}) collective-permute-start(bf16[128,2048]{1,0:T(8,128)(2,1)S(1)} %dynamic-slice_bitcast_fusion), channel_id=1, source_target_pairs={{0,4},{1,5},{2,6},{3,7},{4,0},{5,1},{6,2},{7,3},{8,12},{9,13},{10,... | collective-permute-start | bytes 1572872 | tf_op jit(solution)/shard_map/ppermute | solution.py:16
  5.7 9.3 %collective-permute-start.5 = (bf16[512,256]{1,0:T(8,128)(2,1)}, bf16[512,256]{1,0:T(8,128)(2,1)S(1)}, u32[]{:S(2)}, u32[]{:S(2)}) collective-permute-start(bf16[512,256]{1,0:T(8,128)(2,1)} %bitcast.25), channel_id=1, source_target_pairs={{0,1},{1,0},{2,3},{3,2},{4,5},{5,4},{6,7},{7,6},{8,9},{9,8},{10,11... | collective-permute-start | bytes 786440 | tf_op jit(solution)/shard_map/ppermute | solution.py:16
  8.4 22.2 %copy-start.3 = (bf16[1,512,256]{2,1,0:T(8,128)(2,1)S(1)}, bf16[1,512,256]{2,1,0:T(8,128)(2,1)}, u32[]{:S(2)}) copy-start(bf16[1,512,256]{2,1,0:T(8,128)(2,1)} %param.10) | copy-start | bytes 786436
  8.7 44.8 %collective-permute-start.2 = (bf16[512,1024]{1,0:T(8,128)(2,1)}, bf16[512,1024]{1,0:T(8,128)(2,1)}, u32[]{:S(2)}, u32[]{:S(2)}) collective-permute-start(bf16[512,1024]{1,0:T(8,128)(2,1)} %bitcast.3.w0), channel_id=1, source_target_pairs={{0,2},{1,3},{2,0},{3,1},{4,6},{5,7},{6,4},{7,5},{8,10},{9,11},{10,... | collective-permute-start | bytes 3145736 | tf_op jit(solution)/shard_map/ppermute | solution.py:16
  12.3 18.4 %collective-permute-start.7 = (bf16[512,256]{1,0:T(8,128)(2,1)S(1)}, bf16[512,256]{1,0:T(8,128)(2,1)S(1)}, u32[]{:S(2)}, u32[]{:S(2)}) collective-permute-start(bf16[512,256]{1,0:T(8,128)(2,1)S(1)} %collective-permute-done.6.w2), channel_id=1, source_target_pairs={{0,1},{1,0},{2,3},{3,2},{4,5},{5,4},{6,7},{7,6},{8,9},{9,8},{10,11... | collective-permute-start | bytes 786440 | tf_op jit(solution)/shard_map/ppermute | solution.py:16
  14.7 15.9 %copy-start.8 = (f32[1,4096]{1,0:T(1,128)S(1)}, f32[1,4096]{1,0:T(1,128)}, u32[]{:S(2)}) copy-start(f32[1,4096]{1,0:T(1,128)} %gain_ref.3) | copy-start | bytes 49156
  31.1 12.1 %collective-permute-start.8 = (bf16[128,256]{1,0:T(8,128)(2,1)S(1)}, bf16[128,256]{1,0:T(8,128)(2,1)S(1)}, u32[]{:S(2)}, u32[]{:S(2)}) collective-permute-start(bf16[128,256]{1,0:T(8,128)(2,1)S(1)} %get-tuple-element.21), channel_id=1, source_target_pairs={{0,4},{1,5},{2,6},{3,7},{4,0},{5,1},{6,2},{7,3},{8,12},{9,13},{10,... | collective-permute-start | bytes 196616 | tf_op jit(solution)/shard_map/ppermute | solution.py:16
  33.2 22.4 %copy-start.1 = (bf16[1,1024,512]{2,1,0:T(8,128)(2,1)S(1)}, bf16[1,1024,512]{2,1,0:T(8,128)(2,1)}, u32[]{:S(2)}) copy-start(bf16[1,1024,512]{2,1,0:T(8,128)(2,1)} %param.11) | copy-start | bytes 3145732
  43.3 0.8 copy-start.2
  44.1 44.6 %all-to-all-start = ((bf16[8,128,256]{2,1,0:T(8,128)(2,1)}), bf16[8,128,256]{2,1,0:T(8,128)(2,1)S(1)}, u32[]{:S(2)}, u32[]{:S(2)}) async-start(bf16[8,128,256]{2,1,0:T(8,128)(2,1)} %copy-done.2), calls=%async_computation | async-start | bytes 1048576 | tf_op jit(solution)/shard_map/all_to_all | solution.py:209
  51.2 6.6 %collective-permute-start.1 = (bf16[512,1024]{1,0:T(8,128)(2,1)}, bf16[512,1024]{1,0:T(8,128)(2,1)S(1)}, u32[]{:S(2)}, u32[]{:S(2)}) collective-permute-start(bf16[512,1024]{1,0:T(8,128)(2,1)} %bitcast.3.w0), channel_id=1, source_target_pairs={{0,1},{1,0},{2,3},{3,2},{4,5},{5,4},{6,7},{7,6},{8,9},{9,8},{10,11... | collective-permute-start | bytes 3145736 | tf_op jit(solution)/shard_map/ppermute | solution.py:16
  53.5 4.8 %collective-permute-start.3 = (bf16[512,1024]{1,0:T(8,128)(2,1)}, bf16[512,1024]{1,0:T(8,128)(2,1)S(1)}, u32[]{:S(2)}, u32[]{:S(2)}) collective-permute-start(bf16[512,1024]{1,0:T(8,128)(2,1)} %collective-permute-done.2.w2), channel_id=1, source_target_pairs={{0,1},{1,0},{2,3},{3,2},{4,5},{5,4},{6,7},{7,6},{8,9},{9,8},{10,11... | collective-permute-start | bytes 3145736 | tf_op jit(solution)/shard_map/ppermute | solution.py:16
  55.6 38.1 %collective-permute-start.10 = (bf16[1024,512]{1,0:T(8,128)(2,1)S(1)}, bf16[1024,512]{1,0:T(8,128)(2,1)}, u32[]{:S(2)}, u32[]{:S(2)}) collective-permute-start(bf16[1024,512]{1,0:T(8,128)(2,1)S(1)} %bitcast.19), channel_id=1, source_target_pairs={{0,2},{1,3},{2,0},{3,1},{4,6},{5,7},{6,4},{7,5},{8,10},{9,11},{10,... | collective-permute-start | bytes 3145736 | tf_op jit(solution)/shard_map/ppermute | solution.py:16
  61.1 0.7 copy-start.4
  61.8 26.3 %collective-permute-start.4 = (bf16[128,1024]{1,0:T(8,128)(2,1)S(1)}, bf16[128,1024]{1,0:T(8,128)(2,1)S(1)}, u32[]{:S(2)}, u32[]{:S(2)}) collective-permute-start(bf16[128,1024]{1,0:T(8,128)(2,1)S(1)} %get-tuple-element.19), channel_id=1, source_target_pairs={{0,4},{1,5},{2,6},{3,7},{4,0},{5,1},{6,2},{7,3},{8,12},{9,13},{10,... | collective-permute-start | bytes 786440 | tf_op jit(solution)/shard_map/ppermute | solution.py:16
  64.1 37.4 %collective-permute-start.9 = (bf16[1024,512]{1,0:T(8,128)(2,1)S(1)}, bf16[1024,512]{1,0:T(8,128)(2,1)}, u32[]{:S(2)}, u32[]{:S(2)}) collective-permute-start(bf16[1024,512]{1,0:T(8,128)(2,1)S(1)} %bitcast.20), channel_id=1, source_target_pairs={{0,1},{1,0},{2,3},{3,2},{4,5},{5,4},{6,7},{7,6},{8,9},{9,8},{10,11... | collective-permute-start | bytes 3145736 | tf_op jit(solution)/shard_map/ppermute | solution.py:16
  88.1 0.7 copy-start.6
  88.8 1.0 copy-start.5
  89.7 0.9 copy-start.7
  93.7 7.8 %collective-permute-start.11 = (bf16[1024,512]{1,0:T(8,128)(2,1)}, bf16[1024,512]{1,0:T(8,128)(2,1)S(1)}, u32[]{:S(2)}, u32[]{:S(2)}) collective-permute-start(bf16[1024,512]{1,0:T(8,128)(2,1)} %collective-permute-done.10.refs_5_), channel_id=1, source_target_pairs={{0,1},{1,0},{2,3},{3,2},{4,5},{5,4},{6,7},{7,6},{8,9},{9,8},{10,11... | collective-permute-start | bytes 3145736 | tf_op jit(solution)/shard_map/ppermute | solution.py:16
  96.5 17.5 %collective-permute-start.14 = (bf16[128,1024]{1,0:T(8,128)(2,1)S(1)}, bf16[128,1024]{1,0:T(8,128)(2,1)S(1)}, u32[]{:S(2)}, u32[]{:S(2)}) collective-permute-start(bf16[128,1024]{1,0:T(8,128)(2,1)S(1)} %shard_map.90.refs_1_), channel_id=1, source_target_pairs={{0,4},{1,5},{2,6},{3,7},{4,0},{5,1},{6,2},{7,3},{8,12},{9,13},{10,... | collective-permute-start | bytes 786440 | tf_op jit(solution)/shard_map/ppermute | solution.py:16
  103.9 82.2 %collective-permute-start.12 = (bf16[64,2048]{1,0:T(8,128)(2,1)S(1)}, bf16[64,2048]{1,0:T(8,128)(2,1)S(1)}, u32[]{:S(2)}, u32[]{:S(2)}) collective-permute-start(bf16[64,2048]{1,0:T(8,128)(2,1)S(1)} %get-tuple-element.25), channel_id=1, source_target_pairs={{0,8},{1,9},{2,10},{3,11},{4,12},{5,13},{6,14},{7,15},{8,0},{9,1},... | collective-permute-start | bytes 786440 | tf_op jit(solution)/shard_map/ppermute | solution.py:24
  114.0 8.4 %copy-start.10 = (bf16[1,512,128]{2,1,0:T(8,128)(2,1)S(1)}, bf16[1,512,128]{2,1,0:T(8,128)(2,1)}, u32[]{:S(2)}) copy-start(bf16[1,512,128]{2,1,0:T(8,128)(2,1)} %param.13) | copy-start | bytes 393220
  114.0 80.1 %copy-start.9 = (bf16[1,512,128]{2,1,0:T(8,128)(2,1)S(1)}, bf16[1,512,128]{2,1,0:T(8,128)(2,1)}, u32[]{:S(2)}) copy-start(bf16[1,512,128]{2,1,0:T(8,128)(2,1)} %param.12) | copy-start | bytes 393220
  116.4 81.0 %collective-permute-start.15 = (bf16[128,2048]{1,0:T(8,128)(2,1)S(1)}, bf16[128,2048]{1,0:T(8,128)(2,1)S(1)}, u32[]{:S(2)}, u32[]{:S(2)}) collective-permute-start(bf16[128,2048]{1,0:T(8,128)(2,1)S(1)} %shard_map.92), channel_id=1, source_target_pairs={{0,12},{1,13},{2,14},{3,15},{4,8},{5,9},{6,10},{7,11},{8,4},{9,5},... | collective-permute-start | bytes 1572872 | tf_op jit(solution)/shard_map/ppermute | solution.py:24
  122.4 71.7 %collective-permute-start.16 = (bf16[512,128]{1,0:T(8,128)(2,1)S(1)}, bf16[512,128]{1,0:T(8,128)(2,1)S(1)}, u32[]{:S(2)}, u32[]{:S(2)}) collective-permute-start(bf16[512,128]{1,0:T(8,128)(2,1)S(1)} %bitcast.28), channel_id=1, source_target_pairs={{0,504},{8,496},{16,488},{24,480},{32,472},{40,464},{48,456},{56,4... | collective-permute-start | bytes 393224 | tf_op jit(solution)/shard_map/ppermute | solution.py:230
  186.1 16.9 %collective-permute-start.13 = (bf16[64,2048]{1,0:T(8,128)(2,1)S(1)}, bf16[64,2048]{1,0:T(8,128)(2,1)S(1)}, u32[]{:S(2)}, u32[]{:S(2)}) collective-permute-start(bf16[64,2048]{1,0:T(8,128)(2,1)S(1)} %get-tuple-element.27), channel_id=1, source_target_pairs={{0,8},{1,9},{2,10},{3,11},{4,12},{5,13},{6,14},{7,15},{8,0},{9,1},... | collective-permute-start | bytes 786440 | tf_op jit(solution)/shard_map/ppermute | solution.py:24
